TPU v7x, 512 devices: a whole 4x8x8 slice. The times are simulated.
512 devices in a mesh: dp: 64 (over x, z, core), tensor: 8 (over y).
Axes of the slice: x: 4, y: 8, z: 8, core: 2. Of those that a mesh axis runs over, the one named last changes fastest.
Arguments:
- q_new: bfloat16 [8192, 8192], P(('dp', 'tensor')), may hold values from -6 to 6
- k_new: bfloat16 [8192, 1024], P(('dp', 'tensor')), may hold values from -8 to 8
- v_new: bfloat16 [8192, 1024], P(('dp', 'tensor')), may hold values from -6 to 6
- hist_kv: bfloat16 [2048, 128, 2, 1024], P('dp', None, None, 'tensor'), may hold values from -8 to 8
- sources: int32 [64, 64, 1], P('dp'), may hold values from 0 to 63; in each aligned block of 64 rows (0 to 63, 64 to 127, ..., all dimensions but the last counted through in order) at most 2 rows name the same one
- block_ids: int32 [64, 64], P('dp'), may hold values from 0 to 31
- hist_len: int32 [64], P('dp'), may hold values from 1 to 64, 3840 in all
Outputs:
- attended: bfloat16 [8192, 8192], P(('dp', 'tensor'))
Inputs may be any that keep to these rules, and one draw needn't show every extreme that they name: `sources`: in each group's list no owner is named in more than 2 slots, and some owner is named in exactly 2 slots. `hist_len`: some group has all 64 slots live.
All inputs are finite; a program needn't handle non-finite values.
Results may differ from a plain program's by a relative error of at most 0.0032.
Values may be sent and summed in bfloat16 or wider, within the bound.
No kernel may reach another device: no remote copies, remote signals or barrier semaphores. Data moves between devices by JAX's collectives and lax.ppermute only.
A program may use at most 64 MiB of HBM per device.

v0:
```python
import math

import jax
import jax.numpy as jnp
from jax import lax
from jax.sharding import PartitionSpec as P

HQ = 64
KVH = 8
HD = 128


def slot_ranks(src_rows):
    count = src_rows.shape[-1]
    order = jnp.arange(count)
    earlier = order[None, :] < order[:, None]
    same = (src_rows[..., :, None] == src_rows[..., None, :]) & earlier
    return jnp.sum(same.astype(jnp.int32), axis=-1)


def owner_table(src_rows, id_rows, ranks, owners, capacity):
    match_owner = src_rows[..., None, :] == owners[:, None]
    slot_index = jnp.arange(capacity)
    match_rank = ranks[..., None, :] == slot_index[:, None]
    hitting = match_owner[..., :, None, :] & match_rank[..., None, :, :]
    return jnp.sum(jnp.where(hitting, id_rows[..., None, None, :], 0), axis=-1)


def local(q_new, k_new, v_new, hist_kv, sources, block_ids, hist_len):
    parts = lax.axis_size("tensor")
    groups = lax.axis_size("dp")
    tok_local, q_width = q_new.shape
    kv_width = k_new.shape[1]
    q_parts = q_new.reshape(tok_local, parts, q_width // parts)
    k_parts = k_new.reshape(tok_local, parts, kv_width // parts)
    v_parts = v_new.reshape(tok_local, parts, kv_width // parts)
    q_here, key_local_part, v_here = (
        lax.all_to_all(q_parts, "tensor", split_axis=1, concat_axis=0, tiled=True),
        lax.all_to_all(k_parts, "tensor", split_axis=1, concat_axis=0, tiled=True),
        lax.all_to_all(v_parts, "tensor", split_axis=1, concat_axis=0, tiled=True),
    )
    new_count = q_here.shape[0]
    kv_heads = kv_width // parts // HD
    per_kv = HQ // KVH
    query_rows = q_here.reshape(new_count, kv_heads, per_kv, HD)
    src_list = sources.reshape(-1)
    slots = src_list.shape[0]
    capacity = max(2, 2 * slots // groups)
    ranks = slot_ranks(src_list)
    all_src, all_ids = (
        lax.all_gather(sources, "dp", axis=0, tiled=True),
        lax.all_gather(block_ids, "dp", axis=0, tiled=True),
    )
    all_src = all_src.reshape(groups, slots)
    owners = jnp.reshape(lax.axis_index("dp"), (1,))
    send_table = owner_table(all_src, all_ids, slot_ranks(all_src), owners, capacity).reshape(
        groups, capacity
    )
    picked = hist_kv[send_table.reshape(-1)]
    block_len = picked.shape[1]
    width = picked.shape[3]
    picked = picked.reshape(groups, capacity, block_len, 2, width)
    where_from = src_list * capacity + ranks
    arrived = lax.all_to_all(picked, "dp", split_axis=0, concat_axis=0, tiled=True)
    arrived = arrived.reshape(groups * capacity, block_len, 2, width)[where_from]
    hist_keys = arrived[:, :, 0]
    hist_vals = arrived[:, :, 1]
    score_scale = 1.0 / math.sqrt(HD)
    step = math.gcd(slots, 8)
    turns = slots // step
    key_blocks = hist_keys.reshape(turns, step * block_len, kv_heads, HD)
    val_blocks = hist_vals.reshape(turns, step * block_len, kv_heads, HD)
    live = jnp.repeat((jnp.arange(slots) < hist_len[0]).reshape(turns, step), block_len, axis=1)
    causal = jnp.arange(new_count)[:, None] >= jnp.arange(new_count)[None, :]
    fresh_turn_scores = (
        jnp.einsum("fusi,pui->usfp", query_rows, key_local_part, preferred_element_type=jnp.float32)
        * score_scale
    )
    fresh_turn_scores = jnp.where(causal[None, None], fresh_turn_scores, -jnp.inf)

    def score_block(keys, mask):
        scores = (
            jnp.einsum("nhgd,khd->hgnk", query_rows, keys, preferred_element_type=jnp.float32)
            * score_scale
        )
        return jnp.where(mask[None, None, None, :], scores, -jnp.inf)

    def max_step(top, inputs):
        keys, mask = inputs
        return (jnp.maximum(top, jnp.max(score_block(keys, mask), axis=-1)), None)

    top, _ = lax.scan(max_step, jnp.max(fresh_turn_scores, axis=-1), (key_blocks, live))

    def sum_step(carry, inputs):
        total, running_sum = carry
        keys, vals, mask = inputs
        weights = jnp.exp(score_block(keys, mask) - top[..., None])
        total = total + jnp.sum(weights, axis=-1)
        running_sum = running_sum + jnp.einsum(
            "hgnk,khd->nhgd", weights.astype(jnp.bfloat16), vals, preferred_element_type=jnp.float32
        )
        return ((total, running_sum), None)

    new_weights = jnp.exp(fresh_turn_scores - top[..., None])
    start_total = jnp.sum(new_weights, axis=-1)
    start_summed = jnp.einsum(
        "vxyl,lvq->yvxq",
        new_weights.astype(jnp.bfloat16),
        v_here,
        preferred_element_type=jnp.float32,
    )
    (total, running_sum), _ = lax.scan(
        sum_step, (start_total, start_summed), (key_blocks, val_blocks, live)
    )
    result = running_sum / jnp.transpose(total, (2, 0, 1))[..., None]
    result = result.astype(jnp.bfloat16).reshape(new_count, 1, kv_heads * per_kv * HD)
    back = lax.all_to_all(result, "tensor", split_axis=0, concat_axis=1, tiled=True)
    return back.reshape(tok_local, q_width)


def solution(mesh):
    return jax.shard_map(
        local,
        mesh=mesh,
        in_specs=(
            P(("dp", "tensor"), None),
            P(("dp", "tensor"), None),
            P(("dp", "tensor"), None),
            P("dp", None, None, "tensor"),
            P("dp", None, None),
            P("dp", None),
            P("dp"),
        ),
        out_specs=P(("dp", "tensor"), None),
        check_vma=False,
    )
```

profile of v0, /device:TPU:1, one launch (start us, length us, event | category | flops | bytes accessed | tf_op | source)
XLA Modules:
  0.0 413.8 jit_solution(10428861804598068745)
XLA Ops:
  1.5 7.7 %all-to-all-start = ((bf16[16,8,128]{2,0,1:T(8,128)(2,1)}), bf16[16,8,128]{2,0,1:T(8,128)(2,1)S(1)}, u32[]{:S(2)}, u32[]{:S(2)}) async-start(bf16[16,8,128]{2,0,1:T(8,128)(2,1)} %copy_bitcast_fusion.2), calls=%async_computation | async-start | bytes 65536 | tf_op jit(solution)/shard_map/all_to_all | solution.py:39
  9.2 45.8 %all_gather.6 = s32[64,64,1]{1,2,0:T(1,128)S(1)} all-gather(s32[1,64,1]{1,2,0:T(1,128)} %param.15), channel_id=1, replica_groups=mesh['dp'=64,'tensor'=8] {'dp'}, dimensions={0}, use_global_device_ids=true | all-gather | bytes 16640 | tf_op jit(solution)/shard_map/all_gather | solution.py:51
  56.6 6.9 %all-to-all-start.1 = ((bf16[16,8,1024]{2,0,1:T(8,128)(2,1)}), bf16[16,8,1024]{2,0,1:T(8,128)(2,1)S(1)}, u32[]{:S(2)}, u32[]{:S(2)}) async-start(bf16[16,8,1024]{2,0,1:T(8,128)(2,1)} %bitcast.179), calls=%async_computation.1 | async-start | bytes 524288 | tf_op jit(solution)/shard_map/all_to_all | solution.py:38
  63.6 1.9 convert_reduce_fusion
  65.4 38.3 %all-gather = s32[64,1,64]{2,1,0:T(1,128)S(1)} all-gather(s32[1,1,64]{2,1,0:T(1,128)} %bitcast.232), channel_id=1, replica_groups=mesh['dp'=64,'tensor'=8] {'dp'}, dimensions={0}, use_global_device_ids=true | all-gather | bytes 16640 | tf_op jit(solution)/shard_map/all_gather | solution.py:52
  104.2 19.5 %gather_fusion = bf16[128,128,2,128]{3,2,1,0:T(2,128)(2,1)} fusion(bf16[32,128,2,128]{3,2,1,0:T(2,128)(2,1)S(1)} %copy-done, s32[1024]{0:T(1024)S(1)} %pad_clamp_fusion.1), kind=kCustom, calls=%fused_computation | custom fusion | bytes 16777728 | tf_op jit(solution)/shard_map/gather | solution.py:59
  123.6 9.1 %copy.77 = bf16[64,2,128,2,128]{4,2,3,1,0:T(8,128)(2,1)} copy(bf16[64,2,128,2,128]{4,3,2,1,0:T(2,128)(2,1)} %bitcast.211) | data formatting | bytes 16777216 | tf_op jit(solution)/shard_map/reshape | solution.py:62
  132.8 6.8 %all-to-all-start.2 = ((bf16[64,2,128,2,128]{4,2,3,1,0:T(8,128)(2,1)}), bf16[64,2,128,2,128]{4,2,3,1,0:T(8,128)(2,1)}, u32[]{:S(2)}, u32[]{:S(2)}) async-start(bf16[64,2,128,2,128]{4,2,3,1,0:T(8,128)(2,1)} %copy.77), calls=%async_computation.2 | async-start | bytes 16777216 | tf_op jit(solution)/shard_map/all_to_all | solution.py:64
  141.6 183.8 %all-to-all-done.2 = bf16[64,2,128,2,128]{4,2,3,1,0:T(8,128)(2,1)} async-done(((bf16[64,2,128,2,128]{4,2,3,1,0:T(8,128)(2,1)}), bf16[64,2,128,2,128]{4,2,3,1,0:T(8,128)(2,1)}, u32[]{:S(2)}, u32[]{:S(2)}) %all-to-all-start.2) | async-done | bytes 8388640 | tf_op jit(solution)/shard_map/all_to_all | solution.py:64
  325.4 6.9 %all-to-all-start.3 = ((bf16[16,8,128]{2,0,1:T(8,128)(2,1)}), bf16[16,8,128]{2,0,1:T(8,128)(2,1)S(1)}, u32[]{:S(2)}, u32[]{:S(2)}) async-start(bf16[16,8,128]{2,0,1:T(8,128)(2,1)} %copy_bitcast_fusion.1), calls=%async_computation.3 | async-start | bytes 65536 | tf_op jit(solution)/shard_map/all_to_all | solution.py:40
  332.3 6.4 %gather_fusion.1 = bf16[64,128,2,128]{3,1,2,0:T(8,128)(2,1)} fusion(bf16[128,128,2,128]{3,1,2,0:T(8,128)(2,1)} %bitcast.34, s32[1024]{0:T(1024)S(1)} %pad_clamp_fusion), kind=kCustom, calls=%fused_computation.1 | custom fusion | bytes 8388864 | tf_op jit(solution)/shard_map/gather | solution.py:65
  338.7 4.7 %fusion.39 = (bf16[64,128,1,128]{3,1,2,0:T(8,128)(2,1)}, bf16[64,128,1,128]{3,1,2,0:T(8,128)(2,1)}) fusion(bf16[64,128,2,128]{3,1,2,0:T(8,128)(2,1)} %gather_fusion.1), kind=kLoop, calls=%fused_computation.63 | loop fusion | bytes 8388608 | tf_op jit(solution)/shard_map/slice | solution.py:67
  343.5 14.0 %while.22 = (s32[]{:T(128)}, f32[1,8,128]{2,1,0:T(8,128)S(1)}, pred[8,1024]{1,0:T(8,128)(4,1)S(1)}, bf16[8,1024,1,128]{3,1,2,0:T(8,128)(2,1)}, bf16[128,1,8,128]{3,0,2,1:T(8,128)(2,1)S(1)}, /*index=5*/s32[]{:T(128)}) while((s32[]{:T(128)}, f32[1,8,128]{2,1,0:T(8,128)S(1)}, pred[8,1024]{1,0:T(8,128)(4,1)S(1)}, ...), condition=%wide.region_6.7_spmd, body=%wide.region_4.6_spmd.sunk | while | flops 271581184 | bytes 544329 | solution.py:92
  355.8 1.7 fusion.54
  358.1 34.3 %while.23 = (s32[]{:T(128)}, f32[1,8,128]{2,1,0:T(8,128)S(1)}, f32[128,1,8,128]{0,3,2,1:T(8,128)S(1)}, pred[8,1024]{1,0:T(8,128)(4,1)S(1)}, bf16[8,1024,1,128]{3...) while((s32[]{:T(128)}, f32[1,8,128]{2,1,0:T(8,128)S(1)}, ...), condition=%wide.region_10.11_spmd, body=%wide.region_8.10_spmd.sunk | while | flops 545390592 | bytes 10253409 | solution.py:112
  358.1 2.0 fusion.57
  360.2 2.2 fusion.58
  362.4 2.0 fusion.57
  364.5 2.2 fusion.58
  366.7 2.0 fusion.57
  368.7 2.2 fusion.58
  371.0 2.0 fusion.57
  373.0 2.2 fusion.58
  375.3 2.1 fusion.57
  377.3 2.2 fusion.58
  379.6 2.1 fusion.57
  381.6 2.2 fusion.58
  383.9 2.1 fusion.57
  385.9 2.2 fusion.58
  388.1 2.1 fusion.57
  390.2 2.2 fusion.58
  394.1 18.6 %all_to_all.65 = bf16[8,2,8192]{2,1,0:T(2,128)(2,1)S(1)} all-to-all(bf16[8,2,8192]{2,1,0:T(2,128)(2,1)S(1)} %reshape.256), channel_id=1, replica_groups=mesh['dp'=64,'tensor'=8] {'tensor'}, dimensions={0} | all-to-all | bytes 524288 | tf_op jit(solution)/shard_map/all_to_all | solution.py:117
  (78 shorter events, 20.5 us)
Async XLA Ops:
  0.0 104.1 %copy-start = (bf16[32,128,2,128]{3,2,1,0:T(2,128)(2,1)S(1)}, bf16[32,128,2,128]{3,2,1,0:T(2,128)(2,1)}, u32[]{:S(2)}) copy-start(bf16[32,128,2,128]{3,2,1,0:T(2,128)(2,1)} %param.14) | copy-start | bytes 6291460
  1.5 55.1 %all-to-all-start = ((bf16[16,8,128]{2,0,1:T(8,128)(2,1)}), bf16[16,8,128]{2,0,1:T(8,128)(2,1)S(1)}, u32[]{:S(2)}, u32[]{:S(2)}) async-start(bf16[16,8,128]{2,0,1:T(8,128)(2,1)} %copy_bitcast_fusion.2), calls=%async_computation | async-start | bytes 65536 | tf_op jit(solution)/shard_map/all_to_all | solution.py:39
  56.6 76.1 %all-to-all-start.1 = ((bf16[16,8,1024]{2,0,1:T(8,128)(2,1)}), bf16[16,8,1024]{2,0,1:T(8,128)(2,1)S(1)}, u32[]{:S(2)}, u32[]{:S(2)}) async-start(bf16[16,8,1024]{2,0,1:T(8,128)(2,1)} %bitcast.179), calls=%async_computation.1 | async-start | bytes 524288 | tf_op jit(solution)/shard_map/all_to_all | solution.py:38
  132.8 7.5 %copy-start.2 = (s32[1,64,1]{1,2,0:T(1,128)S(1)}, s32[1,64,1]{1,2,0:T(1,128)}, u32[]{:S(2)}) copy-start(s32[1,64,1]{1,2,0:T(1,128)} %param.15) | copy-start | bytes 772
  132.8 7.8 %copy-start.1 = (bf16[16,1024]{1,0:T(8,128)(2,1)S(1)}, bf16[16,1024]{1,0:T(8,128)(2,1)}, u32[]{:S(2)}) copy-start(bf16[16,1024]{1,0:T(8,128)(2,1)} %param.13) | copy-start | bytes 98308
  132.8 192.6 %all-to-all-start.2 = ((bf16[64,2,128,2,128]{4,2,3,1,0:T(8,128)(2,1)}), bf16[64,2,128,2,128]{4,2,3,1,0:T(8,128)(2,1)}, u32[]{:S(2)}, u32[]{:S(2)}) async-start(bf16[64,2,128,2,128]{4,2,3,1,0:T(8,128)(2,1)} %copy.77), calls=%async_computation.2 | async-start | bytes 16777216 | tf_op jit(solution)/shard_map/all_to_all | solution.py:64
  325.4 32.2 %all-to-all-start.3 = ((bf16[16,8,128]{2,0,1:T(8,128)(2,1)}), bf16[16,8,128]{2,0,1:T(8,128)(2,1)S(1)}, u32[]{:S(2)}, u32[]{:S(2)}) async-start(bf16[16,8,128]{2,0,1:T(8,128)(2,1)} %copy_bitcast_fusion.1), calls=%async_computation.3 | async-start | bytes 65536 | tf_op jit(solution)/shard_map/all_to_all | solution.py:40
where the time goes:
time: 415 us; the launch traced here: 414 us
  waiting for transfers between devices  184 us (44%)
  blocking collectives  103 us (25%)
  matrix products  47.8 us (12%)
  local copies, waits for them, and re-layouts  46.6 us (11%)
  starting transfers between devices  28.3 us (7%)
    all_to_all x1, waiting for transfers between devices, local(): lax.all_to_all(picked, 'dp', split_axis=0, concat_axis=0, tiled=True)  184 us
    all_gather x1, blocking collectives, local(): lax.all_gather(sources, 'dp', axis=0, tiled=True)  45.8 us
    all_gather x1, blocking collectives, local(): lax.all_gather(block_ids, 'dp', axis=0, tiled=True)  38.3 us
    dot_general x16, matrix products, score_block(): jnp.einsum('nhgd,khd->hgnk', query_rows, keys, preferred_element_type=jnp...  29.9 us
    gather x1, local copies, waits for them, and re-layouts, local(): picked = hist_kv[send_table.reshape(-1)]  19.5 us
    all_to_all x1, blocking collectives, local(): lax.all_to_all(result, 'tensor', split_axis=0, concat_axis=1, tiled=True)  18.6 us
    dot_general x8, matrix products, sum_step(): jnp.einsum('hgnk,khd->nhgd', weights.astype(jnp.bfloat16), vals, preferre...  17.4 us
    reshape x1, local copies, waits for them, and re-layouts, local(): picked = picked.reshape(groups, capacity, block_len, 2, width)  9.15 us
  transfers between devices with their start and end apart: 4, of which 1 were waited for; matrix products, arithmetic and copies ran while one was open for 14% of the time, Pallas kernels for 0%

commit v1 on v0

v1 whole, which is shorter than its diff:
```python
import functools
import math

import jax
import jax.numpy as jnp
from jax import lax
from jax.experimental import pallas as pl
from jax.experimental.pallas import tpu as pltpu
from jax.sharding import PartitionSpec as P

HD = 128
CHUNKS = 4
LOG2E = math.log2(math.e)
NEG = -1e30


def gather_kernel(per_step, first, count, piece, rows_ref, table_ref, out_ref):
    step = pl.program_id(0)
    for g in range(per_step):
        for s in range(count):
            row = rows_ref[step * per_step + g, first + s]
            out_ref[g, pl.ds(piece * s, piece), :] = table_ref[row, pl.ds(0, piece), :]
            out_ref[g, pl.ds(piece * (count + s), piece), :] = table_ref[row, pl.ds(piece, piece), :]


def gather_pieces(rows, table, first, count):
    groups = rows.shape[0]
    piece = table.shape[1] // 2
    per_step = min(8, groups)
    return pl.pallas_call(
        functools.partial(gather_kernel, per_step, first, count, piece),
        out_shape=jax.ShapeDtypeStruct((groups, 2 * piece * count, HD), table.dtype),
        grid_spec=pltpu.PrefetchScalarGridSpec(
            num_scalar_prefetch=1,
            grid=(groups // per_step,),
            in_specs=[pl.BlockSpec(table.shape, lambda i, rows: (0, 0, 0))],
            out_specs=pl.BlockSpec((per_step, 2 * piece * count, HD), lambda i, rows: (i, 0, 0)),
        ),
        compiler_params=pltpu.CompilerParams(vmem_limit_bytes=24 << 20),
        cost_estimate=pl.CostEstimate(
            flops=0, transcendentals=0, bytes_accessed=2 * groups * count * 2 * piece * HD * 2
        ),
        name="gather_pieces",
    )(rows, table)


def fold(q, keys, vals, mask, top, total, acc):
    scale = LOG2E / math.sqrt(HD)
    scores = lax.dot_general(q, keys, (((1,), (1,)), ((), ())), preferred_element_type=jnp.float32)
    scores = jnp.where(mask, scores * scale, NEG)
    new_top = jnp.maximum(top, jnp.max(scores, axis=-1, keepdims=True))
    weights = jnp.exp2(scores - new_top)
    shrink = jnp.exp2(top - new_top)
    total = total * shrink + jnp.sum(weights, axis=-1, keepdims=True)
    acc = acc * shrink + jnp.dot(weights.astype(jnp.bfloat16), vals, preferred_element_type=jnp.float32)
    return new_top, total, acc


def attend_kernel(first, count, piece, start, last, len_ref, *refs):
    refs = list(refs)
    qkv_ref, kv_ref = refs[:2]
    refs = refs[2:]
    if not start:
        stat_in, acc_in = refs[:2]
        refs = refs[2:]
    new = qkv_ref.shape[0]
    heads = (qkv_ref.shape[1] - 2 * HD) // HD
    sources = kv_ref.shape[0]
    half = piece * count
    width = sources * half
    keys = kv_ref[:, :half, :].reshape(width, HD)
    vals = kv_ref[:, half:, :].reshape(width, HD)
    slot = first + lax.rem(lax.broadcasted_iota(jnp.int32, (1, width), 1), half) // piece
    live = slot < len_ref[0]
    for h in range(heads):
        cols = pl.ds(h * HD, HD)
        q = qkv_ref[:, cols]
        if start:
            causal = lax.broadcasted_iota(jnp.int32, (new, new), 0) >= lax.broadcasted_iota(
                jnp.int32, (new, new), 1
            )
            state = (
                jnp.full((new, 1), NEG, jnp.float32),
                jnp.zeros((new, 1), jnp.float32),
                jnp.zeros((new, HD), jnp.float32),
            )
            state = fold(
                q, qkv_ref[:, pl.ds(heads * HD, HD)], qkv_ref[:, pl.ds(heads * HD + HD, HD)], causal, *state
            )
        else:
            state = (stat_in[:, pl.ds(2 * h, 1)], stat_in[:, pl.ds(2 * h + 1, 1)], acc_in[:, cols])
        top, total, acc = fold(q, keys, vals, live, *state)
        if last:
            refs[0][:, cols] = (acc / total).astype(jnp.bfloat16)
        else:
            refs[0][:, pl.ds(2 * h, 1)] = top
            refs[0][:, pl.ds(2 * h + 1, 1)] = total
            refs[1][:, cols] = acc


def attend(hist_len, qkv, kv, state, first, count, piece, last):
    new = qkv.shape[0]
    q_width = qkv.shape[1] - 2 * HD
    width = kv.shape[0] * piece * count
    start = state is None
    inputs = (qkv, kv) if start else (qkv, kv, *state)
    if last:
        out_shape = (jax.ShapeDtypeStruct((new, q_width), jnp.bfloat16),)
    else:
        out_shape = (
            jax.ShapeDtypeStruct((new, HD), jnp.float32),
            jax.ShapeDtypeStruct((new, q_width), jnp.float32),
        )
    return pl.pallas_call(
        functools.partial(attend_kernel, first, count, piece, start, last),
        out_shape=out_shape,
        grid_spec=pltpu.PrefetchScalarGridSpec(
            num_scalar_prefetch=1,
            grid=(1,),
            in_specs=[pl.BlockSpec(x.shape, functools.partial(lambda n, i, l: (0,) * n, x.ndim)) for x in inputs],
            out_specs=[pl.BlockSpec(o.shape, lambda i, l: (0, 0)) for o in out_shape],
        ),
        compiler_params=pltpu.CompilerParams(vmem_limit_bytes=40 << 20),
        cost_estimate=pl.CostEstimate(
            flops=4 * new * q_width * width,
            transcendentals=new * q_width // HD * width,
            bytes_accessed=2 * kv.size + 2 * qkv.size,
        ),
        name="attend",
    )(hist_len, *inputs)


def local(q_new, k_new, v_new, hist_kv, sources, block_ids, hist_len):
    parts = lax.axis_size("tensor")
    groups = lax.axis_size("dp")
    tok, q_width = q_new.shape
    kv_width = k_new.shape[1]
    pool, block_len = hist_kv.shape[:2]
    piece = block_len // groups
    slots = block_ids.shape[1]

    spread = hist_kv.reshape(pool, groups, piece, 2, HD)
    spread = jnp.transpose(spread, (1, 0, 3, 2, 4)).reshape(groups, pool * 2 * piece, HD)
    table = lax.all_to_all(spread, "dp", split_axis=0, concat_axis=0, tiled=True)
    table = table.reshape(groups * pool, 2 * piece, HD)

    rows = lax.all_gather(sources.reshape(1, slots) * pool + block_ids, "dp", axis=0, tiled=True)

    qkv = jnp.concatenate(
        [
            q_new.reshape(tok, parts, q_width // parts),
            k_new.reshape(tok, parts, kv_width // parts),
            v_new.reshape(tok, parts, kv_width // parts),
        ],
        axis=-1,
    )
    qkv = jnp.transpose(qkv, (1, 0, 2))
    qkv = lax.all_to_all(qkv, "tensor", split_axis=0, concat_axis=0, tiled=True)
    qkv = qkv.reshape(parts * tok, -1)

    count = slots // CHUNKS
    arrived = []
    for c in range(CHUNKS):
        picked = gather_pieces(rows, table, c * count, count)
        arrived.append(lax.all_to_all(picked, "dp", split_axis=0, concat_axis=0, tiled=True))
    state = None
    for c in range(CHUNKS):
        state = attend(hist_len, qkv, arrived[c], state, c * count, count, piece, c == CHUNKS - 1)
    result = state[0].reshape(parts, tok, q_width // parts)
    back = lax.all_to_all(result, "tensor", split_axis=0, concat_axis=0, tiled=True)
    return jnp.transpose(back, (1, 0, 2)).reshape(tok, q_width)


def solution(mesh):
    return jax.shard_map(
        local,
        mesh=mesh,
        in_specs=(
            P(("dp", "tensor"), None),
            P(("dp", "tensor"), None),
            P(("dp", "tensor"), None),
            P("dp", None, None, "tensor"),
            P("dp", None, None),
            P("dp", None),
            P("dp"),
        ),
        out_specs=P(("dp", "tensor"), None),
        check_vma=False,
    )
```

time: 415 us -> 286 us (0.69)
  waiting for transfers between devices: 184 us -> 130 us
  matrix products: 47.8 us -> 0 us
  blocking collectives: 103 us -> 56.9 us
  Pallas kernels: 0 us -> 42.9 us
  local copies, waits for them, and re-layouts: 46.6 us -> 6.05 us
  starting transfers between devices: 28.3 us -> 47.1 us
    all_to_all x1 -> x4, waiting for transfers between devices: 184 us -> 80.1 us  [local(): lax.all_to_all(picked, 'dp', split_axis=0, concat_axis=0, tiled=True)]
    all_to_all x3 -> x2, waiting for transfers between devices: 0.01 us -> 50.4 us  [the longest x1 50.4 us: local(): lax.all_to_all(spread, 'dp', split_axis=0, concat_axis=0, tiled=True)]
    dot_general x26 -> x0, matrix products: 47.8 us -> none  [the longest x16 29.9 us: score_block(): jnp.einsum('nhgd,khd->hgnk', query_rows, keys, preferred_element_type=jnp...]
    all_gather x2 -> x1, blocking collectives: 84.1 us -> 37.8 us  [local(): lax.all_gather(sources.reshape(1, slots) * pool + block_ids, 'dp', axis=0...]
    pallas_call x0 -> x8, Pallas kernels: none -> 42.9 us  [the longest x4 23.8 us: attend(): pl.pallas_call(functools.partial(attend_kernel, first, count, piece, star...]
    gather x2 -> x0, local copies, waits for them, and re-layouts: 25.9 us -> none  [the longest x1 19.5 us: local(): picked = hist_kv[send_table.reshape(-1)]]
    all_to_all x1 -> x4, starting transfers between devices: 6.83 us -> 25.3 us  [local(): lax.all_to_all(picked, 'dp', split_axis=0, concat_axis=0, tiled=True)]
    reshape x6 -> x3, local copies, waits for them, and re-layouts: 13.5 us -> 0.75 us  [the longest x1 0.72 us: local(): return jnp.transpose(back, (1, 0, 2)).reshape(tok, q_width)]
  transfers between devices with their start and end apart: 4 -> 6, of which waited for: 1 -> 5; matrix products, arithmetic and copies ran while one was open for 14% -> 0% of each run, Pallas kernels for 0% -> 13%
where the time goes in v1:
time: 286 us; the launch traced here: 285 us
  waiting for transfers between devices  130 us (45%)
  blocking collectives  56.9 us (20%)
  starting transfers between devices  47.1 us (16%)
  Pallas kernels  42.9 us (15%)
  local copies, waits for them, and re-layouts  6.05 us (2%)
    all_to_all x4, waiting for transfers between devices, local(): lax.all_to_all(picked, 'dp', split_axis=0, concat_axis=0, tiled=True)  80.1 us
    all_to_all x1, waiting for transfers between devices, local(): lax.all_to_all(spread, 'dp', split_axis=0, concat_axis=0, tiled=True)  50.4 us
    all_gather x1, blocking collectives, local(): lax.all_gather(sources.reshape(1, slots) * pool + block_ids, 'dp', axis=0...  37.8 us
    all_to_all x4, starting transfers between devices, local(): lax.all_to_all(picked, 'dp', split_axis=0, concat_axis=0, tiled=True)  25.3 us
    pallas_call x4, Pallas kernels, attend(): pl.pallas_call(functools.partial(attend_kernel, first, count, piece, star...  23.8 us
    all_to_all x1, blocking collectives, local(): lax.all_to_all(result, 'tensor', split_axis=0, concat_axis=0, tiled=True)  19.1 us
    pallas_call x4, Pallas kernels, gather_pieces(): pl.pallas_call(functools.partial(gather_kernel, per_step, first, count, p...  19.1 us
    all_to_all x1, starting transfers between devices, local(): lax.all_to_all(spread, 'dp', split_axis=0, concat_axis=0, tiled=True)  15 us
  transfers between devices with their start and end apart: 6, of which 5 were waited for; matrix products, arithmetic and copies ran while one was open for 0% of the time, Pallas kernels for 13%

profile of v1, /device:TPU:1, one launch (start us, length us, event | category | flops | bytes accessed | tf_op | source)
XLA Modules:
  0.0 284.9 jit_solution(6046101723094751794)
XLA Ops:
  0.0 0.0 copy-start
  0.0 5.3 %copy.17 = bf16[64,32,2,2,128]{4,3,2,1,0:T(2,128)(2,1)} copy(bf16[64,32,2,2,128]{4,2,3,0,1:T(2,128)(2,1)} %bitcast.47) | data formatting | bytes 4194304 | tf_op jit(solution)/shard_map/transpose | solution.py:143
  5.3 0.0 copy-start.1
  5.3 15.0 %all-to-all-start.1 = ((bf16[64,128,128]{2,1,0:T(8,128)(2,1)}), bf16[64,128,128]{2,1,0:T(8,128)(2,1)S(1)}, u32[]{:S(2)}, u32[]{:S(2)}) async-start(bf16[64,128,128]{2,1,0:T(8,128)(2,1)} %bitcast.46), calls=%async_computation.1 | async-start | bytes 4194304 | tf_op jit(solution)/shard_map/all_to_all | solution.py:144
  20.3 0.0 copy-done.1
  20.3 0.0 copy-done
  20.3 0.0 copy-done.2
  20.4 0.8 maximum_bitcast_fusion
  21.1 50.4 %all-to-all-done.1 = bf16[64,128,128]{2,1,0:T(8,128)(2,1)S(1)} async-done(((bf16[64,128,128]{2,1,0:T(8,128)(2,1)}), bf16[64,128,128]{2,1,0:T(8,128)(2,1)S(1)}, u32[]{:S(2)}, u32[]{:S(2)}) %all-to-all-start.1) | async-done | bytes 2097184 | tf_op jit(solution)/shard_map/all_to_all | solution.py:144
  71.5 6.8 %all-to-all-start = ((bf16[8,16,1280]{2,1,0:T(8,128)(2,1)}), bf16[8,16,1280]{2,1,0:T(8,128)(2,1)S(1)}, u32[]{:S(2)}, u32[]{:S(2)}) async-start(bf16[8,16,1280]{2,1,0:T(8,128)(2,1)} %maximum_bitcast_fusion), calls=%async_computation | async-start | bytes 655360 | tf_op jit(solution)/shard_map/all_to_all | solution.py:158
  78.4 0.0 copy-done.3
  78.4 0.0 copy-done.4
  78.4 37.8 %all-gather = s32[64,1,64]{2,1,0:T(1,128)S(1)} all-gather(s32[1,1,64]{2,1,0:T(1,128)S(1)} %fusion), channel_id=1, replica_groups=mesh['dp'=64,'tensor'=8] {'dp'}, dimensions={0}, use_global_device_ids=true | all-gather | bytes 16640 | tf_op jit(solution)/shard_map/all_gather | solution.py:147
  116.2 4.8 %gather_pieces.7 = bf16[64,64,128]{2,1,0:T(8,128)(2,1)} custom-call(s32[64,64]{1,0:T(8,128)S(1)} %bitcast.37, bf16[2048,4,128]{2,1,0:T(4,128)(2,1)S(1)} %bitcast.33), custom_call_target="tpu_custom_call" | custom-call | bytes 2097152 | tf_op jit(solution)/shard_map/gather_pieces/pallas_call | solution.py:30
  121.0 0.0 all-to-all-done
  121.0 6.1 %all-to-all-start.5 = ((bf16[64,64,128]{2,1,0:T(8,128)(2,1)}), bf16[64,64,128]{2,1,0:T(8,128)(2,1)S(1)}, u32[]{:S(2)}, u32[]{:S(2)}) async-start(bf16[64,64,128]{2,1,0:T(8,128)(2,1)} %gather_pieces.7), calls=%async_computation.5 | async-start | bytes 2097152 | tf_op jit(solution)/shard_map/all_to_all | solution.py:165
  127.1 4.8 %gather_pieces.6 = bf16[64,64,128]{2,1,0:T(8,128)(2,1)} custom-call(s32[64,64]{1,0:T(8,128)S(1)} %bitcast.38, bf16[2048,4,128]{2,1,0:T(4,128)(2,1)S(1)} %bitcast.34), custom_call_target="tpu_custom_call" | custom-call | bytes 2097152 | tf_op jit(solution)/shard_map/gather_pieces/pallas_call | solution.py:30
  131.9 23.8 %all-to-all-done.5.refs_1_ = bf16[64,64,128]{2,1,0:T(8,128)(2,1)S(1)} async-done(((bf16[64,64,128]{2,1,0:T(8,128)(2,1)}), bf16[64,64,128]{2,1,0:T(8,128)(2,1)S(1)}, u32[]{:S(2)}, u32[]{:S(2)}) %all-to-all-start.5) | async-done | bytes 1048608 | tf_op jit(solution)/shard_map/all_to_all | solution.py:165
  155.7 6.4 %all-to-all-start.4 = ((bf16[64,64,128]{2,1,0:T(8,128)(2,1)}), bf16[64,64,128]{2,1,0:T(8,128)(2,1)}, u32[]{:S(2)}, u32[]{:S(2)}) async-start(bf16[64,64,128]{2,1,0:T(8,128)(2,1)} %gather_pieces.6), calls=%async_computation.4 | async-start | bytes 2097152 | tf_op jit(solution)/shard_map/all_to_all | solution.py:165
  162.1 4.8 %gather_pieces.5 = bf16[64,64,128]{2,1,0:T(8,128)(2,1)} custom-call(s32[64,64]{1,0:T(8,128)S(1)} %bitcast.39, bf16[2048,4,128]{2,1,0:T(4,128)(2,1)S(1)} %bitcast.35), custom_call_target="tpu_custom_call" | custom-call | bytes 2097152 | tf_op jit(solution)/shard_map/gather_pieces/pallas_call | solution.py:30
  166.8 23.7 %all-to-all-done.4.refs_1_ = bf16[64,64,128]{2,1,0:T(8,128)(2,1)} async-done(((bf16[64,64,128]{2,1,0:T(8,128)(2,1)}), bf16[64,64,128]{2,1,0:T(8,128)(2,1)}, u32[]{:S(2)}, u32[]{:S(2)}) %all-to-all-start.4) | async-done | bytes 1048608 | tf_op jit(solution)/shard_map/all_to_all | solution.py:165
  190.5 6.4 %all-to-all-start.3 = ((bf16[64,64,128]{2,1,0:T(8,128)(2,1)}), bf16[64,64,128]{2,1,0:T(8,128)(2,1)}, u32[]{:S(2)}, u32[]{:S(2)}) async-start(bf16[64,64,128]{2,1,0:T(8,128)(2,1)} %gather_pieces.5), calls=%async_computation.3 | async-start | bytes 2097152 | tf_op jit(solution)/shard_map/all_to_all | solution.py:165
  196.9 4.8 %gather_pieces.4 = bf16[64,64,128]{2,1,0:T(8,128)(2,1)} custom-call(s32[64,64]{1,0:T(8,128)S(1)} %bitcast.40, bf16[2048,4,128]{2,1,0:T(4,128)(2,1)S(1)} %bitcast.36), custom_call_target="tpu_custom_call" | custom-call | bytes 2097152 | tf_op jit(solution)/shard_map/gather_pieces/pallas_call | solution.py:30
  201.7 23.7 %all-to-all-done.3.refs_1_ = bf16[64,64,128]{2,1,0:T(8,128)(2,1)} async-done(((bf16[64,64,128]{2,1,0:T(8,128)(2,1)}), bf16[64,64,128]{2,1,0:T(8,128)(2,1)}, u32[]{:S(2)}, u32[]{:S(2)}) %all-to-all-start.3) | async-done | bytes 1048608 | tf_op jit(solution)/shard_map/all_to_all | solution.py:165
  225.4 6.4 %all-to-all-start.2 = ((bf16[64,64,128]{2,1,0:T(8,128)(2,1)}), bf16[64,64,128]{2,1,0:T(8,128)(2,1)S(1)}, u32[]{:S(2)}, u32[]{:S(2)}) async-start(bf16[64,64,128]{2,1,0:T(8,128)(2,1)} %gather_pieces.4), calls=%async_computation.2 | async-start | bytes 2097152 | tf_op jit(solution)/shard_map/all_to_all | solution.py:165
  232.4 6.3 %attend.4 = (f32[128,128]{1,0:T(8,128)S(1)}, f32[128,1024]{1,0:T(8,128)S(1)}) custom-call(s32[1]{0:T(128)S(6)} %copy.27.len_ref, bf16[128,1280]{1,0:T(8,128)(2,1)S(1)} %bitcast.41, bf16[64,64,128]{2,1,0:T(8,128)(2,1)S(1)} %all-to-all-done.5.refs_1_), custom_call_target="tpu_custom_call" | custom-call | flops 1073741824 | bytes 1376256 | tf_op jit(solution)/shard_map/attend/pallas_call | solution.py:114
  238.7 6.2 %attend.5 = (f32[128,128]{1,0:T(8,128)S(1)}, f32[128,1024]{1,0:T(8,128)S(1)}) custom-call(s32[1]{0:T(128)S(6)} %copy.27.len_ref, bf16[128,1280]{1,0:T(8,128)(2,1)S(1)} %bitcast.42, bf16[64,64,128]{2,1,0:T(8,128)(2,1)} %all-to-all-done.4.refs_1_, f32[128,128]{1,0:T(8,128)S(1)} %get-tuple-element.11.refs_2_, f32[128,1024]{1,0:T(8,128)S(1)} %get-tuple-element.12.refs_3_), custom_call_target="tpu_custom_call" | custom-call | flops 1073741824 | bytes 1376256 | tf_op jit(solution)/shard_map/attend/pallas_call | solution.py:114
  244.9 6.4 %attend.6 = (f32[128,128]{1,0:T(8,128)S(1)}, f32[128,1024]{1,0:T(8,128)S(1)}) custom-call(s32[1]{0:T(128)S(6)} %copy.27.len_ref, bf16[128,1280]{1,0:T(8,128)(2,1)S(1)} %bitcast.43, bf16[64,64,128]{2,1,0:T(8,128)(2,1)} %all-to-all-done.3.refs_1_, f32[128,128]{1,0:T(8,128)S(1)} %get-tuple-element.13.refs_2_, f32[128,1024]{1,0:T(8,128)S(1)} %get-tuple-element.14.refs_3_), custom_call_target="tpu_custom_call" | custom-call | flops 1073741824 | bytes 1376256 | tf_op jit(solution)/shard_map/attend/pallas_call | solution.py:114
  251.3 8.8 %all-to-all-done.2.refs_1_ = bf16[64,64,128]{2,1,0:T(8,128)(2,1)S(1)} async-done(((bf16[64,64,128]{2,1,0:T(8,128)(2,1)}), bf16[64,64,128]{2,1,0:T(8,128)(2,1)S(1)}, u32[]{:S(2)}, u32[]{:S(2)}) %all-to-all-start.2) | async-done | bytes 1048608 | tf_op jit(solution)/shard_map/all_to_all | solution.py:165
  260.2 5.0 %attend.7 = bf16[128,1024]{1,0:T(8,128)(2,1)S(1)} custom-call(s32[1]{0:T(128)S(6)} %copy.27.len_ref, bf16[128,1280]{1,0:T(8,128)(2,1)S(1)} %bitcast.44, bf16[64,64,128]{2,1,0:T(8,128)(2,1)S(1)} %all-to-all-done.2.refs_1_, f32[128,128]{1,0:T(8,128)S(1)} %get-tuple-element.15.refs_2_, f32[128,1024]{1,0:T(8,128)S(1)} %get-tuple-element.16.refs_3_), custom_call_target="tpu_custom_call" | custom-call | flops 1073741824 | bytes 1376256 | tf_op jit(solution)/shard_map/attend/pallas_call | solution.py:114
  265.1 19.1 %all_to_all.35 = bf16[8,16,1024]{2,1,0:T(8,128)(2,1)S(1)} all-to-all(bf16[8,16,1024]{2,1,0:T(8,128)(2,1)S(1)} %bitcast.45), channel_id=1, replica_groups=mesh['dp'=64,'tensor'=8] {'tensor'}, dimensions={0} | all-to-all | bytes 524288 | tf_op jit(solution)/shard_map/all_to_all | solution.py:170
  284.2 0.7 copy.22
  (6 shorter events, 0.0 us)
Async XLA Ops:
  0.0 20.3 %copy-start = (bf16[16,1024]{1,0:T(8,128)(2,1)S(1)}, bf16[16,1024]{1,0:T(8,128)(2,1)}, u32[]{:S(2)}) copy-start(bf16[16,1024]{1,0:T(8,128)(2,1)} %param.8) | copy-start | bytes 98308
  5.3 15.0 %copy-start.1 = (bf16[16,8192]{1,0:T(8,128)(2,1)S(1)}, bf16[16,8192]{1,0:T(8,128)(2,1)}, u32[]{:S(2)}) copy-start(bf16[16,8192]{1,0:T(8,128)(2,1)} %param.7) | copy-start | bytes 786436
  5.3 15.0 %copy-start.2 = (bf16[16,1024]{1,0:T(8,128)(2,1)S(1)}, bf16[16,1024]{1,0:T(8,128)(2,1)}, u32[]{:S(2)}) copy-start(bf16[16,1024]{1,0:T(8,128)(2,1)} %param.9) | copy-start | bytes 98308
  5.3 73.1 %copy-start.3 = (s32[1,64]{1,0:T(1,128)S(1)}, s32[1,64]{1,0:T(1,128)}, u32[]{:S(2)}) copy-start(s32[1,64]{1,0:T(1,128)} %param.12) | copy-start | bytes 772
  5.3 73.1 %copy-start.4 = (s32[1,64,1]{1,2,0:T(1,128)S(1)}, s32[1,64,1]{1,2,0:T(1,128)}, u32[]{:S(2)}) copy-start(s32[1,64,1]{1,2,0:T(1,128)} %param.11) | copy-start | bytes 772
  5.3 66.2 %all-to-all-start.1 = ((bf16[64,128,128]{2,1,0:T(8,128)(2,1)}), bf16[64,128,128]{2,1,0:T(8,128)(2,1)S(1)}, u32[]{:S(2)}, u32[]{:S(2)}) async-start(bf16[64,128,128]{2,1,0:T(8,128)(2,1)} %bitcast.46), calls=%async_computation.1 | async-start | bytes 4194304 | tf_op jit(solution)/shard_map/all_to_all | solution.py:144
  71.5 49.4 %all-to-all-start = ((bf16[8,16,1280]{2,1,0:T(8,128)(2,1)}), bf16[8,16,1280]{2,1,0:T(8,128)(2,1)S(1)}, u32[]{:S(2)}, u32[]{:S(2)}) async-start(bf16[8,16,1280]{2,1,0:T(8,128)(2,1)} %maximum_bitcast_fusion), calls=%async_computation | async-start | bytes 655360 | tf_op jit(solution)/shard_map/all_to_all | solution.py:158
  121.0 34.7 %all-to-all-start.5 = ((bf16[64,64,128]{2,1,0:T(8,128)(2,1)}), bf16[64,64,128]{2,1,0:T(8,128)(2,1)S(1)}, u32[]{:S(2)}, u32[]{:S(2)}) async-start(bf16[64,64,128]{2,1,0:T(8,128)(2,1)} %gather_pieces.7), calls=%async_computation.5 | async-start | bytes 2097152 | tf_op jit(solution)/shard_map/all_to_all | solution.py:165
  155.7 34.9 %all-to-all-start.4 = ((bf16[64,64,128]{2,1,0:T(8,128)(2,1)}), bf16[64,64,128]{2,1,0:T(8,128)(2,1)}, u32[]{:S(2)}, u32[]{:S(2)}) async-start(bf16[64,64,128]{2,1,0:T(8,128)(2,1)} %gather_pieces.6), calls=%async_computation.4 | async-start | bytes 2097152 | tf_op jit(solution)/shard_map/all_to_all | solution.py:165
  190.5 34.9 %all-to-all-start.3 = ((bf16[64,64,128]{2,1,0:T(8,128)(2,1)}), bf16[64,64,128]{2,1,0:T(8,128)(2,1)}, u32[]{:S(2)}, u32[]{:S(2)}) async-start(bf16[64,64,128]{2,1,0:T(8,128)(2,1)} %gather_pieces.5), calls=%async_computation.3 | async-start | bytes 2097152 | tf_op jit(solution)/shard_map/all_to_all | solution.py:165
  225.4 34.8 %all-to-all-start.2 = ((bf16[64,64,128]{2,1,0:T(8,128)(2,1)}), bf16[64,64,128]{2,1,0:T(8,128)(2,1)S(1)}, u32[]{:S(2)}, u32[]{:S(2)}) async-start(bf16[64,64,128]{2,1,0:T(8,128)(2,1)} %gather_pieces.4), calls=%async_computation.2 | async-start | bytes 2097152 | tf_op jit(solution)/shard_map/all_to_all | solution.py:165

commit v2 on v0

v2 whole, which is shorter than its diff:
```python
import functools
import math

import jax
import jax.numpy as jnp
from jax import lax
from jax.experimental import pallas as pl
from jax.experimental.pallas import tpu as pltpu
from jax.sharding import Mesh
from jax.sharding import PartitionSpec as P

HD = 128
X, Z, C = 4, 8, 2
SCALE = math.log2(math.e) / math.sqrt(HD)
NEG = -1e30
TERMS = 8
TILE = 256
EXTRA = 8


def attend_kernel(start, last, arrays, cap, parts, item_ref, count_ref, home_ref, *refs):
    refs = list(refs)
    stores, refs = refs[:arrays], refs[arrays:]
    q_ref, refs = refs[0], refs[1:]
    if start:
        (key_ref, val_ref), refs = refs[:2], refs[2:]
    else:
        (acc_in, top_in, total_in), refs = refs[:3], refs[3:]
    if last:
        out_ref, buf, scores, top_ref, total_ref, acc_ref, sems = refs
    else:
        acc_out, top_out, total_out, buf, scores, sems = refs
        acc_ref, top_ref, total_ref = acc_out.at[0], top_out.at[0], total_out.at[0]
    group = pl.program_id(0)
    size = stores[0].shape[0]
    rows = parts * HD
    tiles = range(rows // TILE)
    parity = lax.rem(group, 2)
    count = count_ref[group]
    pairs = count // 2
    odd = lax.rem(count, 2)

    def begin(g, par):
        def one(i, _):
            code = item_ref[g, i]
            for a in range(arrays):

                @pl.when(code // size == a)
                def _():
                    pltpu.make_async_copy(stores[a].at[lax.rem(code, size)], buf.at[par, i], sems.at[par, i]).start()

            return 0

        lax.fori_loop(0, count_ref[g], one, 0)

    @pl.when(group == 0)
    def _():
        begin(0, 0)

    @pl.when(group + 1 < pl.num_programs(0))
    def _():
        begin(group + 1, 1 - parity)

    def rows_of(r):
        return pl.ds(r * TILE, TILE)

    def dots(r, keys):
        q = q_ref[0, pl.ds(r * TILE // HD, TILE // HD)].reshape(TILE, HD)
        return lax.dot_general(q, keys, (((1,), (1,)), ((), ())), preferred_element_type=jnp.float32)

    def keys_of(first, many):
        return buf[parity, pl.ds(first, many), 0].reshape(many * HD, HD)

    def vals_of(first, many):
        return buf[parity, pl.ds(first, many), 1].reshape(many * HD, HD)

    if start:
        top_ref[...] = jnp.full(top_ref.shape, NEG, jnp.float32)
        is_home = group == home_ref[0]

        @pl.when(is_home)
        def _():
            keys = key_ref[...].reshape(-1, HD)
            tok = keys.shape[0] // parts
            for r in tiles:
                at = r * TILE + lax.broadcasted_iota(jnp.int32, (TILE, HD), 0)
                token = at // (rows // parts) * tok + lax.rem(at, tok)
                s = jnp.where(lax.broadcasted_iota(jnp.int32, (TILE, HD), 1) <= token, dots(r, keys), NEG)
                scores[cap // 2, rows_of(r), pl.ds(0, HD)] = s
                top_ref[rows_of(r), :] = s

    else:
        top_ref[...] = top_in[0]

    def finish(i, _):
        pltpu.make_async_copy(stores[0].at[0], buf.at[parity, i], sems.at[parity, i]).wait()
        return 0

    lax.fori_loop(0, count, finish, 0)

    def pair_dots(j, _):
        keys = keys_of(2 * j, 2)
        for r in tiles:
            s = dots(r, keys)
            scores[j, rows_of(r), :] = s
            top_ref[rows_of(r), :] = jnp.maximum(top_ref[rows_of(r), :], jnp.maximum(s[:, :HD], s[:, HD:]))
        return 0

    lax.fori_loop(0, pairs, pair_dots, 0)

    @pl.when(odd == 1)
    def _():
        keys = keys_of(count - 1, 1)
        for r in tiles:
            s = dots(r, keys)
            scores[pairs, rows_of(r), pl.ds(0, HD)] = s
            top_ref[rows_of(r), :] = jnp.maximum(top_ref[rows_of(r), :], s)

    for r in tiles:
        top = jnp.max(top_ref[rows_of(r), :], axis=-1, keepdims=True)
        top_ref[rows_of(r), :] = jnp.broadcast_to(top, (TILE, HD))
    if start:
        total_ref[...] = jnp.zeros(total_ref.shape, jnp.float32)
        acc_ref[...] = jnp.zeros(acc_ref.shape, jnp.float32)
    else:
        shrink = jnp.exp2((top_in[0] - top_ref[...]) * SCALE)
        total_ref[...] = total_in[0] * shrink
        acc_ref[...] = acc_in[0] * shrink

    def add(r, w, vals):
        acc_ref[rows_of(r), :] += jnp.dot(w.astype(jnp.bfloat16), vals, preferred_element_type=jnp.float32)

    def single(r, j, vals):
        w = jnp.exp2((scores[j, rows_of(r), pl.ds(0, HD)] - top_ref[rows_of(r), :]) * SCALE)
        total_ref[rows_of(r), :] += w
        add(r, w, vals)

    if start:

        @pl.when(is_home)
        def _():
            for r in tiles:
                single(r, cap // 2, val_ref[...].reshape(-1, HD))

    def pair_sums(j, _):
        vals = vals_of(2 * j, 2)
        for r in tiles:
            top = top_ref[rows_of(r), :]
            w = jnp.exp2((scores[j, rows_of(r), :] - jnp.concatenate([top, top], axis=1)) * SCALE)
            total_ref[rows_of(r), :] += w[:, :HD] + w[:, HD:]
            add(r, w, vals)
        return 0

    lax.fori_loop(0, pairs, pair_sums, 0)

    @pl.when(odd == 1)
    def _():
        for r in tiles:
            single(r, pairs, vals_of(count - 1, 1))

    if not last:
        return
    each = rows // parts
    eye = lax.broadcasted_iota(jnp.int32, (each, HD), 0) == lax.broadcasted_iota(jnp.int32, (each, HD), 1)
    term = lax.broadcasted_iota(jnp.int32, (TERMS, HD), 0)
    for p in range(parts):
        at = pl.ds(p * each, each)
        total = jnp.sum(total_ref[at, :], axis=-1, keepdims=True)
        total = jnp.sum(jnp.where(eye, total, 0.0), axis=0, keepdims=True)
        top = jnp.sum(jnp.where(eye, top_ref[at, :], 0.0), axis=0, keepdims=True)
        some = total > 0
        safe = jnp.where(some, total, 1.0)
        inverse = jnp.where(some, 1.0 / safe, 0.0)
        value = jnp.where(some, top * SCALE + jnp.log2(safe), NEG)
        high = top_bits(value)
        middle = top_bits(value - high)
        low = value - high - middle
        inverse = jnp.transpose(jnp.broadcast_to(inverse, (each, HD)))
        out_ref[p, pl.ds(0, each), :] = (acc_ref[at, :] * inverse).astype(jnp.bfloat16)
        terms = jnp.where(term == 0, high, jnp.where(term == 1, middle, jnp.where(term == 2, low, 0.0)))
        out_ref[p, pl.ds(each, TERMS), :] = terms.astype(jnp.bfloat16)


def top_bits(value):
    shifted = value * 65537.0
    return shifted - (shifted - value)


def attend(items, counts, home, stores, q, kv, state, cap, parts, last):
    groups = q.shape[0]
    rows = parts * HD
    start = state is None

    def block(*s):
        return pl.BlockSpec(s, lambda g, *_: (g,) + (0,) * (len(s) - 1))

    in_specs = [pl.BlockSpec(memory_space=pl.ANY)] * len(stores) + [block(1, parts, HD, HD)]
    inputs = [*stores, q]
    if start:
        heads = kv.shape[2] // (2 * HD)
        tok = HD // parts
        in_specs.append(pl.BlockSpec((parts, tok, HD), lambda g, i, c, h: (0, 0, h[1])))
        in_specs.append(pl.BlockSpec((parts, tok, HD), lambda g, i, c, h: (0, 0, heads + h[1])))
        inputs += [kv, kv]
    else:
        in_specs += [block(1, rows, HD)] * 3
        inputs += list(state)
    scratch = [
        pltpu.VMEM((2, cap, 2, HD, HD), jnp.bfloat16),
        pltpu.VMEM((cap // 2 + int(start), rows, 2 * HD), jnp.float32),
    ]
    if last:
        shape = (groups * parts, rows // parts + TERMS, HD)
        out_shape = [jax.ShapeDtypeStruct(shape, jnp.bfloat16)]
        out_specs = [block(parts, *shape[1:])]
        scratch += [pltpu.VMEM((rows, HD), jnp.float32)] * 3
    else:
        out_shape = [jax.ShapeDtypeStruct((groups, rows, HD), jnp.float32)] * 3
        out_specs = [block(1, rows, HD)] * 3
    work = groups * rows * cap * HD // 2
    return pl.pallas_call(
        functools.partial(attend_kernel, start, last, len(stores), cap, parts),
        out_shape=out_shape,
        grid_spec=pltpu.PrefetchScalarGridSpec(
            num_scalar_prefetch=3,
            grid=(groups,),
            in_specs=in_specs,
            out_specs=out_specs,
            scratch_shapes=scratch + [pltpu.SemaphoreType.DMA((2, cap))],
        ),
        compiler_params=pltpu.CompilerParams(vmem_limit_bytes=60 << 20),
        cost_estimate=pl.CostEstimate(flops=4 * work * HD, transcendentals=work, bytes_accessed=groups * cap * 65536),
        name="attend",
    )(items, counts, home, *inputs)


def combine_kernel(tok, in_ref, out_ref):
    rows = in_ref.shape[2] - TERMS
    spread = jnp.sum(in_ref[:, 0, pl.ds(rows, TERMS), :].astype(jnp.float32), axis=1)
    weights = jnp.exp2(spread - jnp.max(spread, axis=0, keepdims=True))
    weights = jnp.transpose(weights / jnp.sum(weights, axis=0, keepdims=True))
    result = jnp.zeros((rows, HD), jnp.float32)
    for z in range(in_ref.shape[0]):
        result += weights[:, z : z + 1] * in_ref[z, 0, pl.ds(0, rows), :].astype(jnp.float32)
    result = result.astype(jnp.bfloat16)
    for h in range(rows // tok):
        out_ref[:, pl.ds(h * HD, HD)] = result[h * tok : (h + 1) * tok, :]


def combine(partial, tok):
    planes, parts, depth, _ = partial.shape
    width = (depth - TERMS) // tok * HD
    return pl.pallas_call(
        functools.partial(combine_kernel, tok),
        out_shape=jax.ShapeDtypeStruct((tok, parts * width), jnp.bfloat16),
        grid=(parts,),
        in_specs=[pl.BlockSpec((planes, 1, depth, HD), lambda y: (0, y, 0, 0))],
        out_specs=pl.BlockSpec((tok, width), lambda y: (0, y)),
        name="combine",
    )(partial)


def compact(mask, code, cap, filler):
    before = jnp.sum((mask[:, None, :] & jnp.tri(mask.shape[1], k=-1, dtype=bool)[None]).astype(jnp.int32), axis=-1)
    hit = mask[:, None, :] & (before[:, None, :] == jnp.arange(cap)[None, :, None])
    items = jnp.sum(jnp.where(hit, code[:, None, :] - filler, 0), axis=-1) + filler
    return items, jnp.sum(mask.astype(jnp.int32), axis=-1)


def local(q_new, k_new, v_new, hist_kv, sources, block_ids, hist_len):
    parts = lax.axis_size("y")
    planes = lax.axis_size("z")
    x, z, c, y = (lax.axis_index(a) for a in ("x", "z", "c", "y"))
    tok, q_width = q_new.shape
    pool = hist_kv.shape[0]
    half = pool // 2
    slots = block_ids.shape[1]
    up = [(i, (i + 1) % X) for i in range(X)]
    down = [(i, (i - 1) % X) for i in range(X)]
    swap = [(0, 1), (1, 0)]

    own = [jnp.transpose(hist_kv[:half], (0, 2, 1, 3)), jnp.transpose(hist_kv[half:], (0, 2, 1, 3))]
    left = [None, None]
    right = [None, None]
    left[0] = lax.ppermute(own[0], "x", up)
    right[1] = lax.ppermute(own[1], "x", down)
    left[1] = lax.ppermute(own[1], "x", up)
    right[0] = lax.ppermute(own[0], "x", down)
    far = [lax.ppermute(left[0], "x", up), lax.ppermute(right[1], "x", down)]
    q_new, *own = lax.optimization_barrier((q_new, *own))
    own_other, left_other, right_other, far_other = (
        [lax.ppermute(a, "c", swap) for a in pair] for pair in (own, left, right, far)
    )

    heads = q_width // (parts * HD)
    q = jnp.transpose(q_new.reshape(tok, parts, heads, HD), (1, 2, 0, 3)).reshape(parts, heads * tok, HD)
    lists = jnp.concatenate([sources.reshape(1, slots), block_ids, hist_len.reshape(1, 1)], axis=1)
    lists = jnp.pad(lists, ((0, 0), (0, 2 * HD - lists.shape[1]))).reshape(2, HD)
    lists = jnp.pad(lists, ((0, EXTRA - 2), (0, 0))).astype(jnp.bfloat16)
    q = jnp.concatenate([q, jnp.broadcast_to(lists[None], (parts, EXTRA, HD))], axis=1)
    q = jnp.broadcast_to(q[None], (planes, *q.shape)).reshape(planes * parts, *q.shape[1:])
    q = lax.all_to_all(q, ("z", "y"), split_axis=0, concat_axis=0, tiled=True)
    q = q.reshape(planes, parts, *q.shape[1:])

    lists = q[:, 0, HD : HD + 2, :].reshape(planes, 2 * HD).astype(jnp.int32)
    source, block, length = lists[:, :slots], lists[:, slots : 2 * slots], lists[:, 2 * slots : 2 * slots + 1]
    source_x, source_z, other = source // (Z * C), source // C % Z, (source % C != c).astype(jnp.int32)
    step = (source_x - x) % X
    here = (jnp.arange(slots)[None, :] < length) & (source_z == z)
    near_code = (jnp.where(step == 0, 0, jnp.where(step == X - 1, 2, 4)) + other) * pool + block
    near_items, near_counts = compact(here & (step != 2), near_code, 4 * (X - 1), 0)
    far_items, far_counts = compact(here & (step == 2), other * pool + block, 4, 0)

    kv = jnp.pad(jnp.concatenate([k_new, v_new], axis=1), ((0, 3 * tok), (0, 0)))
    kv = lax.all_gather(kv, "y", axis=0, tiled=False)

    home = jnp.stack([z, y])
    near = [*own, *own_other, *left, *left_other, *right, *right_other]
    state = attend(near_items, near_counts, home, near, q, kv, None, 4 * (X - 1), parts, False)
    (partial,) = attend(far_items, far_counts, home, [*far, *far_other], q, None, state, 4, parts, True)
    partial = lax.all_to_all(partial, ("z", "y"), split_axis=0, concat_axis=0, tiled=True)
    return combine(partial.reshape(planes, parts, *partial.shape[1:]), tok)


def solution(mesh):
    mesh = Mesh(mesh.devices.reshape(X, Z, C, -1), ("x", "z", "c", "y"))
    dp = ("x", "z", "c")
    return jax.shard_map(
        local,
        mesh=mesh,
        in_specs=(
            P((*dp, "y"), None),
            P((*dp, "y"), None),
            P((*dp, "y"), None),
            P(dp, None, None, "y"),
            P(dp, None, None),
            P(dp, None),
            P(dp),
        ),
        out_specs=P((*dp, "y"), None),
        check_vma=False,
    )
```

time: 415 us -> 254 us (0.61)
  waiting for transfers between devices: 184 us -> 42.4 us
  matrix products: 47.8 us -> 0 us
  Pallas kernels: 0 us -> 44.2 us
  local copies, waits for them, and re-layouts: 46.6 us -> 8.68 us
  starting transfers between devices: 28.3 us -> 58 us
  blocking collectives: 103 us -> 81.1 us
  between operations: 0.86 us -> 14.5 us
    all_to_all x4 -> x1, waiting for transfers between devices: 184 us -> 0.01 us  [local(): q = lax.all_to_all(q, ('z', 'y'), split_axis=0, concat_axis=0, tiled=True)]
    all_gather x2 -> x0, blocking collectives: 84.1 us -> none  [the longest x1 45.8 us: local(): lax.all_gather(sources, 'dp', axis=0, tiled=True)]
    all_to_all x1, blocking collectives: 18.6 us -> 81.1 us  [local(): lax.all_to_all(partial, ('z', 'y'), split_axis=0, concat_axis=0, tiled=True)]
    dot_general x26 -> x0, matrix products: 47.8 us -> none  [the longest x16 29.9 us: score_block(): jnp.einsum('nhgd,khd->hgnk', query_rows, keys, preferred_element_type=jnp...]
    pallas_call x0 -> x3, Pallas kernels: none -> 44.2 us  [the longest x2 37.6 us: attend(): pl.pallas_call(functools.partial(attend_kernel, start, last, len(stores),...]
    ppermute x0 -> x14, waiting for transfers between devices: none -> 42.4 us  [the longest x1 15.2 us: local(): left[1] = lax.ppermute(own[1], 'x', up)]
    ppermute x0 -> x14, starting transfers between devices: none -> 40.7 us  [the longest x8 21.1 us: local(): lax.ppermute(a, 'c', swap)]
    gather x2 -> x0, local copies, waits for them, and re-layouts: 25.9 us -> none  [the longest x1 19.5 us: local(): picked = hist_kv[send_table.reshape(-1)]]
  transfers between devices with their start and end apart: 4 -> 16, of which waited for: 1 -> 4; matrix products, arithmetic and copies ran while one was open for 14% -> 2% of each run, Pallas kernels for 0% -> 8%
where the time goes in v2:
time: 254 us; the launch traced here: 253 us
  blocking collectives  81.1 us (32%)
  starting transfers between devices  58 us (23%)
  Pallas kernels  44.2 us (17%)
  waiting for transfers between devices  42.4 us (17%)
  between operations  14.5 us (6%)
  local copies, waits for them, and re-layouts  8.68 us (3%)
  other arithmetic  3.99 us (2%)
    all_to_all x1, blocking collectives, local(): lax.all_to_all(partial, ('z', 'y'), split_axis=0, concat_axis=0, tiled=True)  81.1 us
    pallas_call x2, Pallas kernels, attend(): pl.pallas_call(functools.partial(attend_kernel, start, last, len(stores),...  37.6 us
    ppermute x8, starting transfers between devices, local(): lax.ppermute(a, 'c', swap)  21.1 us
    all_to_all x1, starting transfers between devices, local(): q = lax.all_to_all(q, ('z', 'y'), split_axis=0, concat_axis=0, tiled=True)  17.3 us
    ppermute x1, waiting for transfers between devices, local(): left[1] = lax.ppermute(own[1], 'x', up)  15.2 us
    ppermute x2, waiting for transfers between devices, local(): far = [lax.ppermute(left[0], 'x', up), lax.ppermute(right[1], 'x', down)]  13.3 us
    ppermute x1, waiting for transfers between devices, local(): right[1] = lax.ppermute(own[1], 'x', down)  11.6 us
    pallas_call x1, Pallas kernels, combine(): pl.pallas_call(functools.partial(combine_kernel, tok), out_shape=jax.Shap...  6.61 us
  transfers between devices with their start and end apart: 16, of which 4 were waited for; matrix products, arithmetic and copies ran while one was open for 2% of the time, Pallas kernels for 8%

profile of v2, /device:TPU:1, one launch (start us, length us, event | category | flops | bytes accessed | tf_op | source)
XLA Modules:
  0.0 252.9 jit_solution(2335079867869978170)
XLA Ops:
  6.5 2.8 %fusion.18 = (bf16[16,128,2,128]{3,2,1,0:T(2,128)(2,1)S(1)}, bf16[16,128,2,128]{3,2,1,0:T(2,128)(2,1)S(1)}) fusion(bf16[32,128,2,128]{3,2,1,0:T(2,128)(2,1)} %param.10), kind=kLoop, calls=%fused_computation.56 | loop fusion | bytes 4194304 | tf_op jit(solution)/shard_map/slice | solution.py:282
  9.6 1.3 copy.33
  12.0 1.7 broadcast_in_dim.31
  13.7 17.3 %all-to-all-start = ((bf16[64,136,128]{2,1,0:T(8,128)(2,1)}), bf16[64,136,128]{2,1,0:T(8,128)(2,1)S(1)}, u32[]{:S(2)}, u32[]{:S(2)}) async-start(bf16[64,136,128]{2,1,0:T(8,128)(2,1)} %bitcast.32), calls=%async_computation | async-start | bytes 4456448 | tf_op jit(solution)/shard_map/all_to_all | solution.py:302
  31.0 0.7 fusion.2
  31.8 2.9 %collective-permute-start.6 = (bf16[16,2,128,128]{3,2,1,0:T(8,128)(2,1)}, bf16[16,2,128,128]{3,2,1,0:T(8,128)(2,1)S(1)}, u32[]{:S(2)}, u32[]{:S(2)}) collective-permute-start(bf16[16,2,128,128]{3,2,1,0:T(8,128)(2,1)} %bitcast.40), channel_id=1, source_target_pairs={{0,8},{8,0},{1,9},{9,1},{2,10},{10,2},{3,11},{11,3},{4,12},{12,4},... | collective-permute-start | bytes 3145736 | tf_op jit(solution)/shard_map/ppermute | solution.py:292
  34.6 4.4 %collective-permute-start.2 = (bf16[16,2,128,128]{3,2,1,0:T(8,128)(2,1)S(1)}, bf16[16,2,128,128]{3,2,1,0:T(8,128)(2,1)}, u32[]{:S(2)}, u32[]{:S(2)}) collective-permute-start(bf16[16,2,128,128]{3,2,1,0:T(8,128)(2,1)S(1)} %bitcast.36), channel_id=1, source_target_pairs={{0,384},{128,0},{256,128},{384,256},{1,385},{129,1},{257,129},{385... | collective-permute-start | bytes 3145736 | tf_op jit(solution)/shard_map/ppermute | solution.py:286
  39.0 1.9 collective-permute-start
  41.0 2.2 collective-permute-start.7
  43.2 2.4 collective-permute-start.8
  45.6 4.4 %collective-permute-start.11 = (bf16[16,2,128,128]{3,2,1,0:T(8,128)(2,1)}, bf16[16,2,128,128]{3,2,1,0:T(8,128)(2,1)}, u32[]{:S(2)}, u32[]{:S(2)}) collective-permute-start(bf16[16,2,128,128]{3,2,1,0:T(8,128)(2,1)} %bitcast.42), channel_id=1, source_target_pairs={{0,384},{128,0},{256,128},{384,256},{1,385},{129,1},{257,129},{385... | collective-permute-start | bytes 3145736 | tf_op jit(solution)/shard_map/ppermute | solution.py:288
  50.0 11.6 %collective-permute-done.2.refs_9_ = bf16[16,2,128,128]{3,2,1,0:T(8,128)(2,1)} collective-permute-done((bf16[16,2,128,128]{3,2,1,0:T(8,128)(2,1)S(1)}, bf16[16,2,128,128]{3,2,1,0:T(8,128)(2,1)}, u32[]{:S(2)}, u32[]{:S(2)}) %collective-permute-start.2) | collective-permute-done | bytes 1048608 | tf_op jit(solution)/shard_map/ppermute | solution.py:286
  61.6 3.1 %collective-permute-start.13 = (bf16[16,2,128,128]{3,2,1,0:T(8,128)(2,1)}, bf16[16,2,128,128]{3,2,1,0:T(8,128)(2,1)}, u32[]{:S(2)}, u32[]{:S(2)}) collective-permute-start(bf16[16,2,128,128]{3,2,1,0:T(8,128)(2,1)} %collective-permute-done.2.refs_9_), channel_id=1, source_target_pairs={{0,8},{8,0},{1,9},{9,1},{2,10},{10,2},{3,11},{11,3},{4,12},{12,4},... | collective-permute-start | bytes 3145736 | tf_op jit(solution)/shard_map/ppermute | solution.py:292
  64.7 2.2 collective-permute-done.refs_4_
  66.9 1.9 collective-permute-start.1
  68.9 4.6 %collective-permute-start.3 = (bf16[16,2,128,128]{3,2,1,0:T(8,128)(2,1)}, bf16[16,2,128,128]{3,2,1,0:T(8,128)(2,1)}, u32[]{:S(2)}, u32[]{:S(2)}) collective-permute-start(bf16[16,2,128,128]{3,2,1,0:T(8,128)(2,1)} %collective-permute-done.2.refs_9_), channel_id=1, source_target_pairs={{0,384},{128,0},{256,128},{384,256},{1,385},{129,1},{257,129},{385... | collective-permute-start | bytes 3145736 | tf_op jit(solution)/shard_map/ppermute | solution.py:289
  74.2 15.2 %collective-permute-done.8.refs_5_ = bf16[16,2,128,128]{3,2,1,0:T(8,128)(2,1)} collective-permute-done((bf16[16,2,128,128]{3,2,1,0:T(8,128)(2,1)S(1)}, bf16[16,2,128,128]{3,2,1,0:T(8,128)(2,1)}, u32[]{:S(2)}, u32[]{:S(2)}) %collective-permute-start.8) | collective-permute-done | bytes 1048608 | tf_op jit(solution)/shard_map/ppermute | solution.py:287
  89.4 3.7 %collective-permute-start.9 = (bf16[16,2,128,128]{3,2,1,0:T(8,128)(2,1)}, bf16[16,2,128,128]{3,2,1,0:T(8,128)(2,1)}, u32[]{:S(2)}, u32[]{:S(2)}) collective-permute-start(bf16[16,2,128,128]{3,2,1,0:T(8,128)(2,1)} %collective-permute-done.refs_4_), channel_id=1, source_target_pairs={{0,8},{8,0},{1,9},{9,1},{2,10},{10,2},{3,11},{11,3},{4,12},{12,4},... | collective-permute-start | bytes 3145736 | tf_op jit(solution)/shard_map/ppermute | solution.py:292
  93.1 1.9 collective-permute-start.10
  95.1 2.4 collective-permute-start.12
  97.6 1.0 convert_reduce_fusion.2
  98.6 13.3 %collective-permute-done.1.refs_0_ = bf16[16,2,128,128]{3,2,1,0:T(8,128)(2,1)} collective-permute-done((bf16[16,2,128,128]{3,2,1,0:T(8,128)(2,1)}, bf16[16,2,128,128]{3,2,1,0:T(8,128)(2,1)}, u32[]{:S(2)}, u32[]{:S(2)}) %collective-permute-start.1) | collective-permute-done | bytes 1048608 | tf_op jit(solution)/shard_map/ppermute | solution.py:289
  111.9 3.0 %collective-permute-start.4 = (bf16[16,2,128,128]{3,2,1,0:T(8,128)(2,1)}, bf16[16,2,128,128]{3,2,1,0:T(8,128)(2,1)S(1)}, u32[]{:S(2)}, u32[]{:S(2)}) collective-permute-start(bf16[16,2,128,128]{3,2,1,0:T(8,128)(2,1)} %collective-permute-done.1.refs_0_), channel_id=1, source_target_pairs={{0,8},{8,0},{1,9},{9,1},{2,10},{10,2},{3,11},{11,3},{4,12},{12,4},... | collective-permute-start | bytes 3145736 | tf_op jit(solution)/shard_map/ppermute | solution.py:292
  114.9 1.9 collective-permute-start.5
  116.8 0.6 convert_reduce_fusion.3
  118.1 0.7 copy.22.item_ref
  119.0 0.7 copy.23.item_ref
  119.7 20.1 %attend.2 = (f32[8,1024,128]{2,1,0:T(8,128)}, f32[8,1024,128]{2,1,0:T(8,128)}, f32[8,1024,128]{2,1,0:T(8,128)}) custom-call(s32[8,12]{1,0:T(8,128)} %copy.22.item_ref, s32[8]{0:T(128)} %get-tuple-element.19.count_ref, s32[2]{0:T(128)} %pad_add_fusion.home_ref, bf16[16,2,128,128]{3,2,1,0:T(8,128)(2,1)} %bitcast.43, bf16[16,2,128,128]{3,2,1,0:T(8,128)(2,1)} %bitcast.39, ...), custom_call_target="tpu_custom_call" | custom-call | flops 3221225472 | bytes 6291456 | tf_op jit(solution)/shard_map/attend/pallas_call | solution.py:221
  139.9 0.9 copy-done.2
  140.8 17.5 %attend.3 = bf16[64,136,128]{2,1,0:T(8,128)(2,1)} custom-call(s32[8,4]{1,0:T(8,128)} %copy.23.item_ref, s32[8]{0:T(128)} %get-tuple-element.26.count_ref, s32[2]{0:T(128)} %pad_add_fusion.home_ref, bf16[16,2,128,128]{3,2,1,0:T(8,128)(2,1)} %collective-permute-done.1.refs_0_, bf16[16,2,128,128]{3,2,1,0:T(8,128)(2,1)} %collective-permute-done.3.refs_1_, ...), custom_call_target="tpu_custom_call" | custom-call | flops 1073741824 | bytes 2097152 | tf_op jit(solution)/shard_map/attend/pallas_call | solution.py:221
  158.3 81.1 %all_to_all.10 = bf16[64,136,128]{2,1,0:T(8,128)(2,1)} all-to-all(bf16[64,136,128]{2,1,0:T(8,128)(2,1)} %attend.3), channel_id=1, replica_groups=mesh['x'=4,'z'=8,'c'=2,'y'=8] {'z','y'}, dimensions={0} | all-to-all | bytes 4456448 | tf_op jit(solution)/shard_map/all_to_all | solution.py:321
  239.4 6.6 %combine.1 = bf16[16,8192]{1,0:T(8,128)(2,1)} custom-call(bf16[8,8,136,128]{3,2,1,0:T(8,128)(2,1)} %bitcast.33), custom_call_target="tpu_custom_call" | custom-call | tf_op jit(solution)/shard_map/combine/pallas_call | solution.py:253
  (53 shorter events, 2.4 us)
Async XLA Ops:
  9.3 1.6 copy-start.5
  9.3 2.5 copy-start.8
  9.3 2.5 copy-start.9
  9.6 33.6 %copy-start.1 = (bf16[16,128,2,128]{3,1,2,0:T(8,128)(2,1)}, bf16[16,128,2,128]{3,1,2,0:T(8,128)(2,1)S(1)}, u32[]{:S(2)}) copy-start(bf16[16,128,2,128]{3,1,2,0:T(8,128)(2,1)S(1)} %copy.32) | copy-start | bytes 3145732
  13.7 17.3 %copy-start.6 = (bf16[16,1024]{1,0:T(8,128)(2,1)S(1)}, bf16[16,1024]{1,0:T(8,128)(2,1)}, u32[]{:S(2)}) copy-start(bf16[16,1024]{1,0:T(8,128)(2,1)} %param.9) | copy-start | bytes 98308
  13.7 17.3 %copy-start.7 = (bf16[16,1024]{1,0:T(8,128)(2,1)S(1)}, bf16[16,1024]{1,0:T(8,128)(2,1)}, u32[]{:S(2)}) copy-start(bf16[16,1024]{1,0:T(8,128)(2,1)} %param.8) | copy-start | bytes 98308
  13.7 83.8 %all-to-all-start = ((bf16[64,136,128]{2,1,0:T(8,128)(2,1)}), bf16[64,136,128]{2,1,0:T(8,128)(2,1)S(1)}, u32[]{:S(2)}, u32[]{:S(2)}) async-start(bf16[64,136,128]{2,1,0:T(8,128)(2,1)} %bitcast.32), calls=%async_computation | async-start | bytes 4456448 | tf_op jit(solution)/shard_map/all_to_all | solution.py:302
  31.0 88.8 %all-gather.3.cloned.1.call-start = ((), (), s32[]{:S(2)}) async-start(), calls=%async_computation.2 | async-start | bytes 2359296 | tf_op jit(solution)/shard_map/all_gather | solution.py:315
  31.8 13.8 %collective-permute-start.6 = (bf16[16,2,128,128]{3,2,1,0:T(8,128)(2,1)}, bf16[16,2,128,128]{3,2,1,0:T(8,128)(2,1)S(1)}, u32[]{:S(2)}, u32[]{:S(2)}) collective-permute-start(bf16[16,2,128,128]{3,2,1,0:T(8,128)(2,1)} %bitcast.40), channel_id=1, source_target_pairs={{0,8},{8,0},{1,9},{9,1},{2,10},{10,2},{3,11},{11,3},{4,12},{12,4},... | collective-permute-start | bytes 3145736 | tf_op jit(solution)/shard_map/ppermute | solution.py:292
  34.6 27.0 %collective-permute-start.2 = (bf16[16,2,128,128]{3,2,1,0:T(8,128)(2,1)S(1)}, bf16[16,2,128,128]{3,2,1,0:T(8,128)(2,1)}, u32[]{:S(2)}, u32[]{:S(2)}) collective-permute-start(bf16[16,2,128,128]{3,2,1,0:T(8,128)(2,1)S(1)} %bitcast.36), channel_id=1, source_target_pairs={{0,384},{128,0},{256,128},{384,256},{1,385},{129,1},{257,129},{385... | collective-permute-start | bytes 3145736 | tf_op jit(solution)/shard_map/ppermute | solution.py:286
  39.0 27.9 %collective-permute-start = (bf16[16,2,128,128]{3,2,1,0:T(8,128)(2,1)}, bf16[16,2,128,128]{3,2,1,0:T(8,128)(2,1)}, u32[]{:S(2)}, u32[]{:S(2)}) collective-permute-start(bf16[16,2,128,128]{3,2,1,0:T(8,128)(2,1)} %bitcast.41), channel_id=1, source_target_pairs={{0,128},{128,256},{256,384},{384,0},{1,129},{129,257},{257,385},{3... | collective-permute-start | bytes 3145736 | tf_op jit(solution)/shard_map/ppermute | solution.py:285
  41.0 27.9 %collective-permute-start.7 = (bf16[16,2,128,128]{3,2,1,0:T(8,128)(2,1)S(1)}, bf16[16,2,128,128]{3,2,1,0:T(8,128)(2,1)S(1)}, u32[]{:S(2)}, u32[]{:S(2)}) collective-permute-start(bf16[16,2,128,128]{3,2,1,0:T(8,128)(2,1)S(1)} %bitcast.37), channel_id=1, source_target_pairs={{0,8},{8,0},{1,9},{9,1},{2,10},{10,2},{3,11},{11,3},{4,12},{12,4},... | collective-permute-start | bytes 3145736 | tf_op jit(solution)/shard_map/ppermute | solution.py:292
  43.2 46.2 %collective-permute-start.8 = (bf16[16,2,128,128]{3,2,1,0:T(8,128)(2,1)S(1)}, bf16[16,2,128,128]{3,2,1,0:T(8,128)(2,1)}, u32[]{:S(2)}, u32[]{:S(2)}) collective-permute-start(bf16[16,2,128,128]{3,2,1,0:T(8,128)(2,1)S(1)} %bitcast.38), channel_id=1, source_target_pairs={{0,128},{128,256},{256,384},{384,0},{1,129},{129,257},{257,385},{3... | collective-permute-start | bytes 3145736 | tf_op jit(solution)/shard_map/ppermute | solution.py:287
  45.6 23.3 %copy-start.3 = (bf16[16,2,128,128]{3,2,1,0:T(8,128)(2,1)}, bf16[16,2,128,128]{3,2,1,0:T(8,128)(2,1)S(1)}, u32[]{:S(2)}) copy-start(bf16[16,2,128,128]{3,2,1,0:T(8,128)(2,1)S(1)} %collective-permute-done.6.refs_2_) | copy-start | bytes 3145732
  45.6 47.5 %collective-permute-start.11 = (bf16[16,2,128,128]{3,2,1,0:T(8,128)(2,1)}, bf16[16,2,128,128]{3,2,1,0:T(8,128)(2,1)}, u32[]{:S(2)}, u32[]{:S(2)}) collective-permute-start(bf16[16,2,128,128]{3,2,1,0:T(8,128)(2,1)} %bitcast.42), channel_id=1, source_target_pairs={{0,384},{128,0},{256,128},{384,256},{1,385},{129,1},{257,129},{385... | collective-permute-start | bytes 3145736 | tf_op jit(solution)/shard_map/ppermute | solution.py:288
  61.6 33.5 %collective-permute-start.13 = (bf16[16,2,128,128]{3,2,1,0:T(8,128)(2,1)}, bf16[16,2,128,128]{3,2,1,0:T(8,128)(2,1)}, u32[]{:S(2)}, u32[]{:S(2)}) collective-permute-start(bf16[16,2,128,128]{3,2,1,0:T(8,128)(2,1)} %collective-permute-done.2.refs_9_), channel_id=1, source_target_pairs={{0,8},{8,0},{1,9},{9,1},{2,10},{10,2},{3,11},{11,3},{4,12},{12,4},... | collective-permute-start | bytes 3145736 | tf_op jit(solution)/shard_map/ppermute | solution.py:292
  66.9 44.9 %collective-permute-start.1 = (bf16[16,2,128,128]{3,2,1,0:T(8,128)(2,1)}, bf16[16,2,128,128]{3,2,1,0:T(8,128)(2,1)}, u32[]{:S(2)}, u32[]{:S(2)}) collective-permute-start(bf16[16,2,128,128]{3,2,1,0:T(8,128)(2,1)} %collective-permute-done.refs_4_), channel_id=1, source_target_pairs={{0,128},{128,256},{256,384},{384,0},{1,129},{129,257},{257,385},{3... | collective-permute-start | bytes 3145736 | tf_op jit(solution)/shard_map/ppermute | solution.py:289
  68.9 4.6 %copy-start.4 = (bf16[16,2,128,128]{3,2,1,0:T(8,128)(2,1)}, bf16[16,2,128,128]{3,2,1,0:T(8,128)(2,1)S(1)}, u32[]{:S(2)}) copy-start(bf16[16,2,128,128]{3,2,1,0:T(8,128)(2,1)S(1)} %collective-permute-done.7.refs_3_) | copy-start | bytes 3145732
  68.9 46.0 %collective-permute-start.3 = (bf16[16,2,128,128]{3,2,1,0:T(8,128)(2,1)}, bf16[16,2,128,128]{3,2,1,0:T(8,128)(2,1)}, u32[]{:S(2)}, u32[]{:S(2)}) collective-permute-start(bf16[16,2,128,128]{3,2,1,0:T(8,128)(2,1)} %collective-permute-done.2.refs_9_), channel_id=1, source_target_pairs={{0,384},{128,0},{256,128},{384,256},{1,385},{129,1},{257,129},{385... | collective-permute-start | bytes 3145736 | tf_op jit(solution)/shard_map/ppermute | solution.py:289
  89.4 30.3 %collective-permute-start.9 = (bf16[16,2,128,128]{3,2,1,0:T(8,128)(2,1)}, bf16[16,2,128,128]{3,2,1,0:T(8,128)(2,1)}, u32[]{:S(2)}, u32[]{:S(2)}) collective-permute-start(bf16[16,2,128,128]{3,2,1,0:T(8,128)(2,1)} %collective-permute-done.refs_4_), channel_id=1, source_target_pairs={{0,8},{8,0},{1,9},{9,1},{2,10},{10,2},{3,11},{11,3},{4,12},{12,4},... | collective-permute-start | bytes 3145736 | tf_op jit(solution)/shard_map/ppermute | solution.py:292
  93.1 26.6 %collective-permute-start.10 = (bf16[16,2,128,128]{3,2,1,0:T(8,128)(2,1)}, bf16[16,2,128,128]{3,2,1,0:T(8,128)(2,1)}, u32[]{:S(2)}, u32[]{:S(2)}) collective-permute-start(bf16[16,2,128,128]{3,2,1,0:T(8,128)(2,1)} %collective-permute-done.8.refs_5_), channel_id=1, source_target_pairs={{0,8},{8,0},{1,9},{9,1},{2,10},{10,2},{3,11},{11,3},{4,12},{12,4},... | collective-permute-start | bytes 3145736 | tf_op jit(solution)/shard_map/ppermute | solution.py:292
  95.1 24.6 %collective-permute-start.12 = (bf16[16,2,128,128]{3,2,1,0:T(8,128)(2,1)}, bf16[16,2,128,128]{3,2,1,0:T(8,128)(2,1)}, u32[]{:S(2)}, u32[]{:S(2)}) collective-permute-start(bf16[16,2,128,128]{3,2,1,0:T(8,128)(2,1)} %collective-permute-done.11.refs_8_), channel_id=1, source_target_pairs={{0,8},{8,0},{1,9},{9,1},{2,10},{10,2},{3,11},{11,3},{4,12},{12,4},... | collective-permute-start | bytes 3145736 | tf_op jit(solution)/shard_map/ppermute | solution.py:292
  97.5 22.2 %copy-start = (bf16[64,136,128]{2,1,0:T(8,128)(2,1)}, bf16[64,136,128]{2,1,0:T(8,128)(2,1)S(1)}, u32[]{:S(2)}) copy-start(bf16[64,136,128]{2,1,0:T(8,128)(2,1)S(1)} %all-to-all-done) | copy-start | bytes 6684676
  111.9 28.0 %collective-permute-start.4 = (bf16[16,2,128,128]{3,2,1,0:T(8,128)(2,1)}, bf16[16,2,128,128]{3,2,1,0:T(8,128)(2,1)S(1)}, u32[]{:S(2)}, u32[]{:S(2)}) collective-permute-start(bf16[16,2,128,128]{3,2,1,0:T(8,128)(2,1)} %collective-permute-done.1.refs_0_), channel_id=1, source_target_pairs={{0,8},{8,0},{1,9},{9,1},{2,10},{10,2},{3,11},{11,3},{4,12},{12,4},... | collective-permute-start | bytes 3145736 | tf_op jit(solution)/shard_map/ppermute | solution.py:292
  114.9 25.0 %collective-permute-start.5 = (bf16[16,2,128,128]{3,2,1,0:T(8,128)(2,1)}, bf16[16,2,128,128]{3,2,1,0:T(8,128)(2,1)}, u32[]{:S(2)}, u32[]{:S(2)}) collective-permute-start(bf16[16,2,128,128]{3,2,1,0:T(8,128)(2,1)} %collective-permute-done.3.refs_1_), channel_id=1, source_target_pairs={{0,8},{8,0},{1,9},{9,1},{2,10},{10,2},{3,11},{11,3},{4,12},{12,4},... | collective-permute-start | bytes 3145736 | tf_op jit(solution)/shard_map/ppermute | solution.py:292
  139.9 1.0 copy-start.2
Sparse Core Ops, SparseCore 0:
  33.9 68.9 all-gather.2

commit v3 on v2

v3 whole, which is shorter than its diff:
```python
import functools
import math

import jax
import jax.numpy as jnp
from jax import lax
from jax.experimental import pallas as pl
from jax.experimental.pallas import tpu as pltpu
from jax.sharding import Mesh
from jax.sharding import PartitionSpec as P

HD = 128
X, Z, C = 4, 8, 2
SCALE = math.log2(math.e) / math.sqrt(HD)
NEG = -1e30
TERMS = 8
LIMIT = 4000.0
FINE = float(1 << 18)
SHY = 1.0 - 2.0**-13
TILE = 256
EXTRA = 8


def attend_kernel(arrays, cap, parts, item_ref, count_ref, home_ref, *refs):
    stores = refs[:arrays]
    q_ref, key_ref, val_ref, out_ref, buf, scores, top_ref, total_ref, acc_ref, sems = refs[arrays:]
    group = pl.program_id(0)
    rows = acc_ref.shape[0]
    tiles = range(rows // TILE)
    parity = lax.rem(group, 2)
    count = count_ref[group]

    def begin(g, par):
        def one(i, _):
            code = item_ref[g, i]
            store, block = code >> 8, code & 255

            def pick(low, high):
                if high - low == 1:
                    pltpu.make_async_copy(stores[low].at[block], buf.at[par, i], sems.at[par, i]).start()
                    return
                middle = (low + high) // 2
                pl.when(store < middle)(lambda: pick(low, middle))
                pl.when(store >= middle)(lambda: pick(middle, high))

            pick(0, arrays)
            return 0

        lax.fori_loop(0, count_ref[g], one, 0)

    @pl.when(group == 0)
    def _():
        begin(0, 0)

    @pl.when(group + 1 < pl.num_programs(0))
    def _():
        begin(group + 1, 1 - parity)

    def rows_of(r):
        return pl.ds(r * TILE, TILE)

    def dots(r, keys):
        return lax.dot_general(
            q_ref[0, rows_of(r), :], keys, (((1,), (1,)), ((), ())), preferred_element_type=jnp.float32
        )

    def keys_of(first, many):
        return buf[parity, pl.ds(first, many), 0].reshape(many * HD, HD)

    def vals_of(first, many):
        return buf[parity, pl.ds(first, many), 1].reshape(many * HD, HD)

    top_ref[...] = jnp.full(top_ref.shape, NEG, jnp.float32)
    is_home = group == home_ref[0]

    @pl.when(is_home)
    def _():
        keys = key_ref[...].reshape(-1, HD)
        tok = keys.shape[0] // parts
        for r in tiles:
            at = r * TILE + lax.broadcasted_iota(jnp.int32, (TILE, HD), 0)
            token = at // (rows // parts) * tok + lax.rem(at, tok)
            s = jnp.where(lax.broadcasted_iota(jnp.int32, (TILE, HD), 1) <= token, dots(r, keys), NEG)
            scores[cap, rows_of(r), :] = s
            top_ref[rows_of(r), :] = s

    def finish(i, _):
        pltpu.make_async_copy(stores[0].at[0], buf.at[parity, i], sems.at[parity, i]).wait()
        return 0

    lax.fori_loop(0, count, finish, 0)

    def in_steps(step):
        quads = count >> 2
        lax.fori_loop(0, quads, lambda j, _: (step(4 * j, 4), 0)[1], 0)
        pl.when(count & 2 != 0)(lambda: step(4 * quads, 2))
        pl.when(count & 1 != 0)(lambda: step(count - 1, 1))

    def dots_step(first, many):
        keys = keys_of(first, many)
        for r in tiles:
            s = dots(r, keys)
            top = top_ref[rows_of(r), :]
            for i in range(many):
                part = s[:, i * HD : (i + 1) * HD]
                scores[first + i, rows_of(r), :] = part
                top = jnp.maximum(top, part)
            top_ref[rows_of(r), :] = top

    in_steps(dots_step)
    for r in tiles:
        top = jnp.max(top_ref[rows_of(r), :], axis=-1, keepdims=True)
        top_ref[rows_of(r), :] = jnp.broadcast_to(top, (TILE, HD))
    total_ref[...] = jnp.zeros(total_ref.shape, jnp.float32)
    acc_ref[...] = jnp.zeros(acc_ref.shape, jnp.float32)

    def sums(r, first, many, vals):
        top = top_ref[rows_of(r), :]
        w = [jnp.exp2((scores[first + i, rows_of(r), :] - top) * SCALE) for i in range(many)]
        total_ref[rows_of(r), :] += sum(w)
        w = [a.astype(jnp.bfloat16) for a in w]
        w = w[0] if many == 1 else jnp.concatenate(w, axis=1)
        acc_ref[rows_of(r), :] += jnp.dot(w, vals, preferred_element_type=jnp.float32)

    @pl.when(is_home)
    def _():
        for r in tiles:
            sums(r, cap, 1, val_ref[...].reshape(-1, HD))

    def sums_step(first, many):
        vals = vals_of(first, many)
        for r in tiles:
            sums(r, first, many, vals)

    in_steps(sums_step)
    each = rows // parts
    eye = lax.broadcasted_iota(jnp.int32, (each, HD), 0) == lax.broadcasted_iota(jnp.int32, (each, HD), 1)
    term = lax.broadcasted_iota(jnp.int32, (TERMS, HD), 0)
    for p in range(parts):
        at = pl.ds(p * each, each)
        total = jnp.sum(total_ref[at, :], axis=-1, keepdims=True)
        total = jnp.sum(jnp.where(eye, total, 0.0), axis=0, keepdims=True)
        top = jnp.sum(jnp.where(eye, top_ref[at, :], 0.0), axis=0, keepdims=True)
        some = total > 0
        safe = jnp.where(some, total, 1.0)
        inverse = jnp.where(some, 1.0 / safe, 0.0)
        value = jnp.where(some, top * SCALE + jnp.log2(safe), NEG)
        inverse = jnp.transpose(jnp.broadcast_to(inverse, (each, HD)))
        result = acc_ref[at, :] * inverse
        largest = jnp.max(jnp.max(jnp.abs(result), axis=0, keepdims=True), axis=1, keepdims=True)
        power = jnp.clip(jnp.floor(jnp.log2(largest)) + 1.0, -100.0, 15.0)
        fixed = result * (jnp.exp2(15.0 - power) * SHY)
        out_ref[p, pl.ds(0, each), :] = fixed.astype(jnp.int32).astype(jnp.int16)
        value = jnp.floor(jnp.clip(value, -LIMIT, LIMIT) * FINE + 0.5).astype(jnp.int32)
        power = jnp.broadcast_to(power, (1, HD)).astype(jnp.int32)
        terms = jnp.where(term == 0, value >> 16, jnp.where(term == 1, (value & 65535) - 32768, power))
        out_ref[p, pl.ds(each, TERMS), :] = terms.astype(jnp.int16)


def attend(items, counts, home, stores, q, fresh, cap):
    groups = q.shape[0]
    parts, depth, _ = fresh.shape
    rows = parts * HD
    tok = (depth - HD) // 2

    def fresh_block(at):
        return pl.BlockSpec((parts, tok, HD), lambda g, *_: (0, HD // tok + at, 0))

    shape = (groups * parts, rows // parts + TERMS, HD)
    work = groups * rows * cap * HD // 2
    return pl.pallas_call(
        functools.partial(attend_kernel, len(stores), cap, parts),
        out_shape=jax.ShapeDtypeStruct(shape, jnp.int16),
        grid_spec=pltpu.PrefetchScalarGridSpec(
            num_scalar_prefetch=3,
            grid=(groups,),
            in_specs=[
                *[pl.BlockSpec(memory_space=pl.ANY)] * len(stores),
                pl.BlockSpec((1, rows, HD), lambda g, *_: (g, 0, 0)),
                fresh_block(0),
                fresh_block(1),
            ],
            out_specs=pl.BlockSpec((parts, *shape[1:]), lambda g, *_: (g, 0, 0)),
            scratch_shapes=[
                pltpu.VMEM((2, cap, 2, HD, HD), jnp.bfloat16),
                pltpu.VMEM((cap + 1, rows, HD), jnp.float32),
                pltpu.VMEM((rows, HD), jnp.float32),
                pltpu.VMEM((rows, HD), jnp.float32),
                pltpu.VMEM((rows, HD), jnp.float32),
                pltpu.SemaphoreType.DMA((2, cap)),
            ],
        ),
        compiler_params=pltpu.CompilerParams(vmem_limit_bytes=60 << 20),
        cost_estimate=pl.CostEstimate(flops=4 * work * HD, transcendentals=work, bytes_accessed=groups * cap * 65536),
        name="attend",
    )(items, counts, home, *stores, q, fresh, fresh)


def combine_kernel(tok, in_ref, out_ref):
    rows = in_ref.shape[2] - TERMS
    terms = in_ref[:, 0, pl.ds(rows, TERMS), :].astype(jnp.int32)
    spread = (terms[:, 0, :] * 65536 + terms[:, 1, :] + 32768).astype(jnp.float32) * (1.0 / FINE)
    weights = jnp.exp2(spread - jnp.max(spread, axis=0, keepdims=True))
    weights = weights / jnp.sum(weights, axis=0, keepdims=True)
    weights = jnp.transpose(weights * (jnp.exp2(terms[:, 2, :].astype(jnp.float32) - 15.0) / SHY))
    result = jnp.zeros((rows, HD), jnp.float32)
    for z in range(in_ref.shape[0]):
        result += weights[:, z : z + 1] * in_ref[z, 0, pl.ds(0, rows), :].astype(jnp.int32).astype(jnp.float32)
    result = result.astype(jnp.bfloat16)
    for h in range(rows // tok):
        out_ref[:, pl.ds(h * HD, HD)] = result[h * tok : (h + 1) * tok, :]


def combine(partial, tok):
    planes, parts, depth, _ = partial.shape
    width = (depth - TERMS) // tok * HD
    return pl.pallas_call(
        functools.partial(combine_kernel, tok),
        out_shape=jax.ShapeDtypeStruct((tok, parts * width), jnp.bfloat16),
        grid=(parts,),
        in_specs=[pl.BlockSpec((planes, 1, depth, HD), lambda y: (0, y, 0, 0))],
        out_specs=pl.BlockSpec((tok, width), lambda y: (0, y)),
        name="combine",
    )(partial)


def compact(mask, code, cap, filler):
    before = jnp.sum((mask[:, None, :] & jnp.tri(mask.shape[1], k=-1, dtype=bool)[None]).astype(jnp.int32), axis=-1)
    hit = mask[:, None, :] & (before[:, None, :] == jnp.arange(cap)[None, :, None])
    items = jnp.sum(jnp.where(hit, code[:, None, :] - filler, 0), axis=-1) + filler
    return items, jnp.sum(mask.astype(jnp.int32), axis=-1)


def local(q_new, k_new, v_new, hist_kv, sources, block_ids, hist_len):
    parts = lax.axis_size("y")
    planes = lax.axis_size("z")
    x, z, c, y = (lax.axis_index(a) for a in ("x", "z", "c", "y"))
    tok, q_width = q_new.shape
    pool = hist_kv.shape[0]
    half = pool // 2
    slots = block_ids.shape[1]
    up = [(i, (i + 1) % X) for i in range(X)]
    down = [(i, (i - 1) % X) for i in range(X)]
    swap = [(0, 1), (1, 0)]

    own = [jnp.transpose(hist_kv[:half], (0, 2, 1, 3)), jnp.transpose(hist_kv[half:], (0, 2, 1, 3))]
    left = [None, None]
    right = [None, None]
    left[0] = lax.ppermute(own[0], "x", up)
    right[1] = lax.ppermute(own[1], "x", down)
    left[1] = lax.ppermute(own[1], "x", up)
    right[0] = lax.ppermute(own[0], "x", down)
    far = [lax.ppermute(left[0], "x", up), lax.ppermute(right[1], "x", down)]
    heads = q_width // (parts * HD)
    fresh = jnp.concatenate(
        [
            jnp.transpose(a.reshape(tok, parts, -1, HD), (1, 2, 0, 3)).reshape(parts, -1, HD)
            for a in (q_new, k_new, v_new)
        ],
        axis=1,
    )
    fresh = lax.all_to_all(fresh, "y", split_axis=0, concat_axis=0, tiled=True)
    lists = jnp.concatenate([sources.reshape(1, slots), block_ids, hist_len.reshape(1, 1)], axis=1)
    lists = jnp.pad(lists, ((0, 0), (0, EXTRA * HD - lists.shape[1]))).reshape(EXTRA, HD).astype(jnp.bfloat16)
    rows = parts * heads * tok
    q = jnp.concatenate([fresh[:, : heads * tok].reshape(rows, HD), lists], axis=0)
    q, near_left, near_right = lax.optimization_barrier((q, left[0], right[1]))
    q = lax.all_gather(q, "z", axis=0, tiled=False)
    own_other, left_other, right_other, far_other = (
        [lax.ppermute(a, "c", swap) for a in pair] for pair in (own, (near_left, left[1]), (right[0], near_right), far)
    )

    lists = q[:, rows : rows + 2, :].reshape(planes, 2 * HD).astype(jnp.int32)
    source, block, length = lists[:, :slots], lists[:, slots : 2 * slots], lists[:, 2 * slots : 2 * slots + 1]
    source_x, source_z, other = source // (Z * C), source // C % Z, (source % C != c).astype(jnp.int32)
    step = (source_x - x) % X
    here = (jnp.arange(slots)[None, :] < length) & (source_z == z)
    code = (2 * (2 * step + other) + block // half) * 256 + block % half
    items, counts = compact(here, code, 4 * X, 0)
    stores = [*own, *own_other, *right, *right_other, *far, *far_other, *left, *left_other]
    partial = attend(items, counts, z.reshape(1), stores, q, fresh, 4 * X)
    partial = lax.all_to_all(partial, ("z", "y"), split_axis=0, concat_axis=0, tiled=True)
    return combine(partial.reshape(planes, parts, *partial.shape[1:]), tok)


def solution(mesh):
    mesh = Mesh(mesh.devices.reshape(X, Z, C, -1), ("x", "z", "c", "y"))
    dp = ("x", "z", "c")
    return jax.shard_map(
        local,
        mesh=mesh,
        in_specs=(
            P((*dp, "y"), None),
            P((*dp, "y"), None),
            P((*dp, "y"), None),
            P(dp, None, None, "y"),
            P(dp, None, None),
            P(dp, None),
            P(dp),
        ),
        out_specs=P((*dp, "y"), None),
        check_vma=False,
    )
```

time: 254 us -> 229 us (0.902)
  the two profiles are of different devices: /device:TPU:1 before, /device:TPU:6 now
where the time goes in v3:
time: 229 us; the launch traced here: 228 us
  blocking collectives  81.2 us (35%)
  waiting for transfers between devices  45.2 us (20%)
  starting transfers between devices  42.4 us (19%)
  Pallas kernels  36.2 us (16%)
  between operations  14.5 us (6%)
  local copies, waits for them, and re-layouts  4.64 us (2%)
  other arithmetic  4.23 us (2%)
    all_to_all x1, blocking collectives, local(): lax.all_to_all(partial, ('z', 'y'), split_axis=0, concat_axis=0, tiled=True)  81.2 us
    pallas_call x1, Pallas kernels, attend(): pl.pallas_call(functools.partial(attend_kernel, len(stores), cap, parts),...  29.6 us
    ppermute x2, waiting for transfers between devices, local(): far = [lax.ppermute(left[0], 'x', up), lax.ppermute(right[1], 'x', down)]  18.2 us
    ppermute x8, starting transfers between devices, local(): lax.ppermute(a, 'c', swap)  16.2 us
    ppermute x1, waiting for transfers between devices, local(): right[0] = lax.ppermute(own[0], 'x', down)  12.7 us
    all_to_all x1, waiting for transfers between devices, local(): fresh = lax.all_to_all(fresh, 'y', split_axis=0, concat_axis=0, tiled=True)  11.7 us
    ppermute x1, starting transfers between devices, local(): left[0] = lax.ppermute(own[0], 'x', up)  7.76 us
    pallas_call x1, Pallas kernels, combine(): pl.pallas_call(functools.partial(combine_kernel, tok), out_shape=jax.Shap...  6.63 us
  transfers between devices with their start and end apart: 16, of which 5 were waited for; matrix products, arithmetic and copies ran while one was open for 2% of the time, Pallas kernels for 0%

profile of v3, /device:TPU:6, one launch (start us, length us, event | category | flops | bytes accessed | tf_op | source)
XLA Modules:
  0.0 228.3 jit_solution(7586300402662133725)
XLA Ops:
  6.5 2.7 %fusion.22 = (bf16[16,128,2,128]{3,2,1,0:T(2,128)(2,1)S(1)}, bf16[16,128,2,128]{3,2,1,0:T(2,128)(2,1)S(1)}) fusion(bf16[32,128,2,128]{3,2,1,0:T(2,128)(2,1)} %param.10), kind=kLoop, calls=%fused_computation.61 | loop fusion | bytes 4194304 | tf_op jit(solution)/shard_map/slice | solution.py:246
  9.3 0.2 copy.37
  9.5 7.8 %collective-permute-start = (bf16[16,2,128,128]{3,2,1,0:T(8,128)(2,1)S(1)}, bf16[16,2,128,128]{3,2,1,0:T(8,128)(2,1)S(1)}, u32[]{:S(2)}, u32[]{:S(2)}) collective-permute-start(bf16[16,2,128,128]{3,2,1,0:T(8,128)(2,1)S(1)} %bitcast.43), channel_id=1, source_target_pairs={{0,128},{128,256},{256,384},{384,0},{1,129},{129,257},{257,385},{3... | collective-permute-start | bytes 3145736 | tf_op jit(solution)/shard_map/ppermute | solution.py:249
  17.3 0.2 copy.36
  17.6 1.9 collective-permute-start.1
  19.8 0.8 pad_maximum_fusion
  20.6 3.4 %all-to-all-start = ((bf16[8,160,128]{2,1,0:T(8,128)(2,1)}), bf16[8,160,128]{2,1,0:T(8,128)(2,1)S(1)}, u32[]{:S(2)}, u32[]{:S(2)}) async-start(bf16[8,160,128]{2,1,0:T(8,128)(2,1)} %pad_maximum_fusion), calls=%async_computation | async-start | bytes 655360 | tf_op jit(solution)/shard_map/all_to_all | solution.py:262
  24.8 11.7 %all-to-all-done.refs_17_.refs_18_ = bf16[8,160,128]{2,1,0:T(8,128)(2,1)S(1)} async-done(((bf16[8,160,128]{2,1,0:T(8,128)(2,1)}), bf16[8,160,128]{2,1,0:T(8,128)(2,1)S(1)}, u32[]{:S(2)}, u32[]{:S(2)}) %all-to-all-start) | async-done | bytes 327712 | tf_op jit(solution)/shard_map/all_to_all | solution.py:262
  36.6 0.8 pad_maximum_fusion.1
  37.4 2.5 %collective-permute-done.1.refs_5_ = bf16[16,2,128,128]{3,2,1,0:T(8,128)(2,1)} collective-permute-done((bf16[16,2,128,128]{3,2,1,0:T(8,128)(2,1)S(1)}, bf16[16,2,128,128]{3,2,1,0:T(8,128)(2,1)}, u32[]{:S(2)}, u32[]{:S(2)}) %collective-permute-start.1) | collective-permute-done | bytes 1048608 | tf_op jit(solution)/shard_map/ppermute | solution.py:250
  39.9 2.4 %collective-permute-start.4 = (bf16[16,2,128,128]{3,2,1,0:T(8,128)(2,1)S(1)}, bf16[16,2,128,128]{3,2,1,0:T(8,128)(2,1)}, u32[]{:S(2)}, u32[]{:S(2)}) collective-permute-start(bf16[16,2,128,128]{3,2,1,0:T(8,128)(2,1)S(1)} %bitcast.44), channel_id=1, source_target_pairs={{0,384},{128,0},{256,128},{384,256},{1,385},{129,1},{257,129},{385... | collective-permute-start | bytes 3145736 | tf_op jit(solution)/shard_map/ppermute | solution.py:252
  42.3 1.9 collective-permute-start.2
  44.2 4.6 %collective-permute-start.11 = (bf16[16,2,128,128]{3,2,1,0:T(8,128)(2,1)S(1)}, bf16[16,2,128,128]{3,2,1,0:T(8,128)(2,1)}, u32[]{:S(2)}, u32[]{:S(2)}) collective-permute-start(bf16[16,2,128,128]{3,2,1,0:T(8,128)(2,1)S(1)} %bitcast.48), channel_id=1, source_target_pairs={{0,128},{128,256},{256,384},{384,0},{1,129},{129,257},{257,385},{3... | collective-permute-start | bytes 3145736 | tf_op jit(solution)/shard_map/ppermute | solution.py:251
  48.9 2.1 collective-permute-start.3
  51.0 12.7 %collective-permute-done.4.refs_4_ = bf16[16,2,128,128]{3,2,1,0:T(8,128)(2,1)} collective-permute-done((bf16[16,2,128,128]{3,2,1,0:T(8,128)(2,1)S(1)}, bf16[16,2,128,128]{3,2,1,0:T(8,128)(2,1)}, u32[]{:S(2)}, u32[]{:S(2)}) %collective-permute-start.4) | collective-permute-done | bytes 1048608 | tf_op jit(solution)/shard_map/ppermute | solution.py:252
  63.7 1.9 collective-permute-start.5
  65.6 4.0 %collective-permute-start.7 = (bf16[16,2,128,128]{3,2,1,0:T(8,128)(2,1)S(1)}, bf16[16,2,128,128]{3,2,1,0:T(8,128)(2,1)}, u32[]{:S(2)}, u32[]{:S(2)}) collective-permute-start(bf16[16,2,128,128]{3,2,1,0:T(8,128)(2,1)S(1)} %collective-permute-done.refs_12_), channel_id=1, source_target_pairs={{0,128},{128,256},{256,384},{384,0},{1,129},{129,257},{257,385},{3... | collective-permute-start | bytes 3145736 | tf_op jit(solution)/shard_map/ppermute | solution.py:253
  69.7 1.1 copy-done.4
  70.7 1.9 collective-permute-start.8
  72.7 2.1 collective-permute-start.6
  74.8 2.2 collective-permute-start.12
  77.0 2.1 collective-permute-start.13
  79.2 15.2 %collective-permute-done.7.refs_8_ = bf16[16,2,128,128]{3,2,1,0:T(8,128)(2,1)} collective-permute-done((bf16[16,2,128,128]{3,2,1,0:T(8,128)(2,1)S(1)}, bf16[16,2,128,128]{3,2,1,0:T(8,128)(2,1)}, u32[]{:S(2)}, u32[]{:S(2)}) %collective-permute-start.7) | collective-permute-done | bytes 1048608 | tf_op jit(solution)/shard_map/ppermute | solution.py:253
  94.4 1.9 collective-permute-start.9
  96.3 3.0 %collective-permute-done.8.refs_9_ = bf16[16,2,128,128]{3,2,1,0:T(8,128)(2,1)S(1)} collective-permute-done((bf16[16,2,128,128]{3,2,1,0:T(8,128)(2,1)}, bf16[16,2,128,128]{3,2,1,0:T(8,128)(2,1)S(1)}, u32[]{:S(2)}, u32[]{:S(2)}) %collective-permute-start.8) | collective-permute-done | bytes 1048608 | tf_op jit(solution)/shard_map/ppermute | solution.py:253
  99.3 1.9 collective-permute-start.10
  101.3 0.7 convert_bitcast_fusion
  102.2 0.7 convert_reduce_fusion.1
  103.1 0.8 select_reduce_fusion.item_ref
  104.0 29.6 %attend.1 = s16[64,136,128]{2,1,0:T(8,128)(2,1)} custom-call(s32[8,16]{1,0:T(8,128)} %select_reduce_fusion.item_ref, s32[8]{0:T(128)} %get-tuple-element.11.count_ref, s32[1]{0:T(128)} %bitcast.13.home_ref, bf16[16,2,128,128]{3,2,1,0:T(8,128)(2,1)} %bitcast.46, bf16[16,2,128,128]{3,2,1,0:T(8,128)(2,1)} %bitcast.50, bf16[16,2,128,128]{3,2,1,0:T(8,128)(2,1)} %copy-done.4, ...), custom_call_target="tpu_custom_call" | custom-call | flops 4294967296 | bytes 8388608 | tf_op jit(solution)/shard_map/attend/pallas_call | solution.py:171
  133.6 81.2 %all_to_all.10 = s16[64,136,128]{2,1,0:T(8,128)(2,1)} all-to-all(s16[64,136,128]{2,1,0:T(8,128)(2,1)} %attend.1), channel_id=1, replica_groups=mesh['x'=4,'z'=8,'c'=2,'y'=8] {'z','y'}, dimensions={0} | all-to-all | bytes 4456448 | tf_op jit(solution)/shard_map/all_to_all | solution.py:282
  214.9 6.6 %combine.1 = bf16[16,8192]{1,0:T(8,128)(2,1)} custom-call(s16[8,8,136,128]{3,2,1,0:T(8,128)(2,1)} %bitcast.42), custom_call_target="tpu_custom_call" | custom-call | tf_op jit(solution)/shard_map/combine/pallas_call | solution.py:217
  (50 shorter events, 1.0 us)
Async XLA Ops:
  9.2 10.3 %copy-start.7 = (bf16[16,1024]{1,0:T(8,128)(2,1)S(1)}, bf16[16,1024]{1,0:T(8,128)(2,1)}, u32[]{:S(2)}) copy-start(bf16[16,1024]{1,0:T(8,128)(2,1)} %param.8) | copy-start | bytes 98308
  9.2 10.3 %copy-start.8 = (bf16[16,1024]{1,0:T(8,128)(2,1)S(1)}, bf16[16,1024]{1,0:T(8,128)(2,1)}, u32[]{:S(2)}) copy-start(bf16[16,1024]{1,0:T(8,128)(2,1)} %param.9) | copy-start | bytes 98308
  9.2 10.3 %copy-start.6 = (bf16[16,8192]{1,0:T(8,128)(2,1)S(1)}, bf16[16,8192]{1,0:T(8,128)(2,1)}, u32[]{:S(2)}) copy-start(bf16[16,8192]{1,0:T(8,128)(2,1)} %param.7) | copy-start | bytes 786436
  9.5 32.8 %copy-start.1 = (bf16[16,128,2,128]{3,1,2,0:T(8,128)(2,1)}, bf16[16,128,2,128]{3,1,2,0:T(8,128)(2,1)S(1)}, u32[]{:S(2)}) copy-start(bf16[16,128,2,128]{3,1,2,0:T(8,128)(2,1)S(1)} %copy.37) | copy-start | bytes 3145732
  9.5 27.9 %collective-permute-start = (bf16[16,2,128,128]{3,2,1,0:T(8,128)(2,1)S(1)}, bf16[16,2,128,128]{3,2,1,0:T(8,128)(2,1)S(1)}, u32[]{:S(2)}, u32[]{:S(2)}) collective-permute-start(bf16[16,2,128,128]{3,2,1,0:T(8,128)(2,1)S(1)} %bitcast.43), channel_id=1, source_target_pairs={{0,128},{128,256},{256,384},{384,0},{1,129},{129,257},{257,385},{3... | collective-permute-start | bytes 3145736 | tf_op jit(solution)/shard_map/ppermute | solution.py:249
  17.3 7.4 %copy-start.9 = (s32[1,64]{1,0:T(1,128)S(1)}, s32[1,64]{1,0:T(1,128)}, u32[]{:S(2)}) copy-start(s32[1,64]{1,0:T(1,128)} %param.12) | copy-start | bytes 772
  17.3 7.4 %copy-start.10 = (s32[1,64,1]{1,2,0:T(1,128)S(1)}, s32[1,64,1]{1,2,0:T(1,128)}, u32[]{:S(2)}) copy-start(s32[1,64,1]{1,2,0:T(1,128)} %param.11) | copy-start | bytes 772
  17.6 86.4 %copy-start.2 = (bf16[16,128,2,128]{3,1,2,0:T(8,128)(2,1)}, bf16[16,128,2,128]{3,1,2,0:T(8,128)(2,1)S(1)}, u32[]{:S(2)}) copy-start(bf16[16,128,2,128]{3,1,2,0:T(8,128)(2,1)S(1)} %copy.36) | copy-start | bytes 3145732
  17.6 22.3 %collective-permute-start.1 = (bf16[16,2,128,128]{3,2,1,0:T(8,128)(2,1)S(1)}, bf16[16,2,128,128]{3,2,1,0:T(8,128)(2,1)}, u32[]{:S(2)}, u32[]{:S(2)}) collective-permute-start(bf16[16,2,128,128]{3,2,1,0:T(8,128)(2,1)S(1)} %bitcast.47), channel_id=1, source_target_pairs={{0,384},{128,0},{256,128},{384,256},{1,385},{129,1},{257,129},{385... | collective-permute-start | bytes 3145736 | tf_op jit(solution)/shard_map/ppermute | solution.py:250
  20.6 16.0 %all-to-all-start = ((bf16[8,160,128]{2,1,0:T(8,128)(2,1)}), bf16[8,160,128]{2,1,0:T(8,128)(2,1)S(1)}, u32[]{:S(2)}, u32[]{:S(2)}) async-start(bf16[8,160,128]{2,1,0:T(8,128)(2,1)} %pad_maximum_fusion), calls=%async_computation | async-start | bytes 655360 | tf_op jit(solution)/shard_map/all_to_all | solution.py:262
  24.0 77.3 %all-gather.3.cloned.1.call-start = ((), (), s32[]{:S(2)}) async-start(), calls=%async_computation.2 | async-start | bytes 2377728 | tf_op jit(solution)/shard_map/all_gather | solution.py:268
  36.6 67.4 %copy-start = (bf16[8,160,128]{2,1,0:T(8,128)(2,1)}, bf16[8,160,128]{2,1,0:T(8,128)(2,1)S(1)}, u32[]{:S(2)}) copy-start(bf16[8,160,128]{2,1,0:T(8,128)(2,1)S(1)} %all-to-all-done.refs_17_.refs_18_) | copy-start | bytes 983044
  37.4 66.6 %copy-start.3 = (bf16[16,2,128,128]{3,2,1,0:T(8,128)(2,1)}, bf16[16,2,128,128]{3,2,1,0:T(8,128)(2,1)S(1)}, u32[]{:S(2)}) copy-start(bf16[16,2,128,128]{3,2,1,0:T(8,128)(2,1)S(1)} %collective-permute-done.refs_12_) | copy-start | bytes 3145732
  39.9 23.8 %collective-permute-start.4 = (bf16[16,2,128,128]{3,2,1,0:T(8,128)(2,1)S(1)}, bf16[16,2,128,128]{3,2,1,0:T(8,128)(2,1)}, u32[]{:S(2)}, u32[]{:S(2)}) collective-permute-start(bf16[16,2,128,128]{3,2,1,0:T(8,128)(2,1)S(1)} %bitcast.44), channel_id=1, source_target_pairs={{0,384},{128,0},{256,128},{384,256},{1,385},{129,1},{257,129},{385... | collective-permute-start | bytes 3145736 | tf_op jit(solution)/shard_map/ppermute | solution.py:252
  42.3 27.3 %collective-permute-start.2 = (bf16[16,2,128,128]{3,2,1,0:T(8,128)(2,1)S(1)}, bf16[16,2,128,128]{3,2,1,0:T(8,128)(2,1)S(1)}, u32[]{:S(2)}, u32[]{:S(2)}) collective-permute-start(bf16[16,2,128,128]{3,2,1,0:T(8,128)(2,1)S(1)} %bitcast.45), channel_id=1, source_target_pairs={{0,8},{8,0},{1,9},{9,1},{2,10},{10,2},{3,11},{11,3},{4,12},{12,4},... | collective-permute-start | bytes 3145736 | tf_op jit(solution)/shard_map/ppermute | solution.py:270
  44.2 28.4 %collective-permute-start.11 = (bf16[16,2,128,128]{3,2,1,0:T(8,128)(2,1)S(1)}, bf16[16,2,128,128]{3,2,1,0:T(8,128)(2,1)}, u32[]{:S(2)}, u32[]{:S(2)}) collective-permute-start(bf16[16,2,128,128]{3,2,1,0:T(8,128)(2,1)S(1)} %bitcast.48), channel_id=1, source_target_pairs={{0,128},{128,256},{256,384},{384,0},{1,129},{129,257},{257,385},{3... | collective-permute-start | bytes 3145736 | tf_op jit(solution)/shard_map/ppermute | solution.py:251
  48.9 25.9 %collective-permute-start.3 = (bf16[16,2,128,128]{3,2,1,0:T(8,128)(2,1)S(1)}, bf16[16,2,128,128]{3,2,1,0:T(8,128)(2,1)}, u32[]{:S(2)}, u32[]{:S(2)}) collective-permute-start(bf16[16,2,128,128]{3,2,1,0:T(8,128)(2,1)S(1)} %bitcast.49), channel_id=1, source_target_pairs={{0,8},{8,0},{1,9},{9,1},{2,10},{10,2},{3,11},{11,3},{4,12},{12,4},... | collective-permute-start | bytes 3145736 | tf_op jit(solution)/shard_map/ppermute | solution.py:270
  63.7 13.3 %collective-permute-start.5 = (bf16[16,2,128,128]{3,2,1,0:T(8,128)(2,1)}, bf16[16,2,128,128]{3,2,1,0:T(8,128)(2,1)}, u32[]{:S(2)}, u32[]{:S(2)}) collective-permute-start(bf16[16,2,128,128]{3,2,1,0:T(8,128)(2,1)} %collective-permute-done.4.refs_4_), channel_id=1, source_target_pairs={{0,8},{8,0},{1,9},{9,1},{2,10},{10,2},{3,11},{11,3},{4,12},{12,4},... | collective-permute-start | bytes 3145736 | tf_op jit(solution)/shard_map/ppermute | solution.py:270
  65.6 28.8 %collective-permute-start.7 = (bf16[16,2,128,128]{3,2,1,0:T(8,128)(2,1)S(1)}, bf16[16,2,128,128]{3,2,1,0:T(8,128)(2,1)}, u32[]{:S(2)}, u32[]{:S(2)}) collective-permute-start(bf16[16,2,128,128]{3,2,1,0:T(8,128)(2,1)S(1)} %collective-permute-done.refs_12_), channel_id=1, source_target_pairs={{0,128},{128,256},{256,384},{384,0},{1,129},{129,257},{257,385},{3... | collective-permute-start | bytes 3145736 | tf_op jit(solution)/shard_map/ppermute | solution.py:253
  69.6 1.1 copy-start.4
  70.7 28.6 %collective-permute-start.8 = (bf16[16,2,128,128]{3,2,1,0:T(8,128)(2,1)}, bf16[16,2,128,128]{3,2,1,0:T(8,128)(2,1)S(1)}, u32[]{:S(2)}, u32[]{:S(2)}) collective-permute-start(bf16[16,2,128,128]{3,2,1,0:T(8,128)(2,1)} %collective-permute-done.1.refs_5_), channel_id=1, source_target_pairs={{0,384},{128,0},{256,128},{384,256},{1,385},{129,1},{257,129},{385... | collective-permute-start | bytes 3145736 | tf_op jit(solution)/shard_map/ppermute | solution.py:253
  72.7 31.3 %collective-permute-start.6 = (bf16[16,2,128,128]{3,2,1,0:T(8,128)(2,1)}, bf16[16,2,128,128]{3,2,1,0:T(8,128)(2,1)}, u32[]{:S(2)}, u32[]{:S(2)}) collective-permute-start(bf16[16,2,128,128]{3,2,1,0:T(8,128)(2,1)} %collective-permute-done.1.refs_5_), channel_id=1, source_target_pairs={{0,8},{8,0},{1,9},{9,1},{2,10},{10,2},{3,11},{11,3},{4,12},{12,4},... | collective-permute-start | bytes 3145736 | tf_op jit(solution)/shard_map/ppermute | solution.py:270
  74.8 29.1 %collective-permute-start.12 = (bf16[16,2,128,128]{3,2,1,0:T(8,128)(2,1)S(1)}, bf16[16,2,128,128]{3,2,1,0:T(8,128)(2,1)}, u32[]{:S(2)}, u32[]{:S(2)}) collective-permute-start(bf16[16,2,128,128]{3,2,1,0:T(8,128)(2,1)S(1)} %collective-permute-done.refs_12_), channel_id=1, source_target_pairs={{0,8},{8,0},{1,9},{9,1},{2,10},{10,2},{3,11},{11,3},{4,12},{12,4},... | collective-permute-start | bytes 3145736 | tf_op jit(solution)/shard_map/ppermute | solution.py:270
  77.0 26.9 %collective-permute-start.13 = (bf16[16,2,128,128]{3,2,1,0:T(8,128)(2,1)}, bf16[16,2,128,128]{3,2,1,0:T(8,128)(2,1)}, u32[]{:S(2)}, u32[]{:S(2)}) collective-permute-start(bf16[16,2,128,128]{3,2,1,0:T(8,128)(2,1)} %collective-permute-done.11.refs_13_), channel_id=1, source_target_pairs={{0,8},{8,0},{1,9},{9,1},{2,10},{10,2},{3,11},{11,3},{4,12},{12,4},... | collective-permute-start | bytes 3145736 | tf_op jit(solution)/shard_map/ppermute | solution.py:270
  94.4 9.6 %collective-permute-start.9 = (bf16[16,2,128,128]{3,2,1,0:T(8,128)(2,1)}, bf16[16,2,128,128]{3,2,1,0:T(8,128)(2,1)}, u32[]{:S(2)}, u32[]{:S(2)}) collective-permute-start(bf16[16,2,128,128]{3,2,1,0:T(8,128)(2,1)} %collective-permute-done.7.refs_8_), channel_id=1, source_target_pairs={{0,8},{8,0},{1,9},{9,1},{2,10},{10,2},{3,11},{11,3},{4,12},{12,4},... | collective-permute-start | bytes 3145736 | tf_op jit(solution)/shard_map/ppermute | solution.py:270
  99.3 4.7 %copy-start.5 = (bf16[16,2,128,128]{3,2,1,0:T(8,128)(2,1)}, bf16[16,2,128,128]{3,2,1,0:T(8,128)(2,1)S(1)}, u32[]{:S(2)}) copy-start(bf16[16,2,128,128]{3,2,1,0:T(8,128)(2,1)S(1)} %collective-permute-done.8.refs_9_) | copy-start | bytes 3145732
  99.3 4.7 %collective-permute-start.10 = (bf16[16,2,128,128]{3,2,1,0:T(8,128)(2,1)S(1)}, bf16[16,2,128,128]{3,2,1,0:T(8,128)(2,1)}, u32[]{:S(2)}, u32[]{:S(2)}) collective-permute-start(bf16[16,2,128,128]{3,2,1,0:T(8,128)(2,1)S(1)} %collective-permute-done.8.refs_9_), channel_id=1, source_target_pairs={{0,8},{8,0},{1,9},{9,1},{2,10},{10,2},{3,11},{11,3},{4,12},{12,4},... | collective-permute-start | bytes 3145736 | tf_op jit(solution)/shard_map/ppermute | solution.py:270
Sparse Core Ops, SparseCore 0:
  40.0 48.9 all-gather.2

commit v4 on v3

--- a/solution.py
+++ b/solution.py
@@ -198,28 +198,30 @@
 
 def combine_kernel(tok, in_ref, out_ref):
     rows = in_ref.shape[2] - TERMS
-    terms = in_ref[:, 0, pl.ds(rows, TERMS), :].astype(jnp.int32)
-    spread = (terms[:, 0, :] * 65536 + terms[:, 1, :] + 32768).astype(jnp.float32) * (1.0 / FINE)
-    weights = jnp.exp2(spread - jnp.max(spread, axis=0, keepdims=True))
-    weights = weights / jnp.sum(weights, axis=0, keepdims=True)
-    weights = jnp.transpose(weights * (jnp.exp2(terms[:, 2, :].astype(jnp.float32) - 15.0) / SHY))
-    result = jnp.zeros((rows, HD), jnp.float32)
-    for z in range(in_ref.shape[0]):
-        result += weights[:, z : z + 1] * in_ref[z, 0, pl.ds(0, rows), :].astype(jnp.int32).astype(jnp.float32)
-    result = result.astype(jnp.bfloat16)
-    for h in range(rows // tok):
-        out_ref[:, pl.ds(h * HD, HD)] = result[h * tok : (h + 1) * tok, :]
-
-
-def combine(partial, tok):
+    heads = rows // tok
+    for y in range(in_ref.shape[1]):
+        terms = in_ref[:, y, pl.ds(rows, TERMS), :].astype(jnp.int32)
+        spread = (terms[:, 0, :] * 65536 + terms[:, 1, :] + 32768).astype(jnp.float32) * (1.0 / FINE)
+        weights = jnp.exp2(spread - jnp.max(spread, axis=0, keepdims=True))
+        weights = weights / jnp.sum(weights, axis=0, keepdims=True)
+        weights = jnp.transpose(weights * (jnp.exp2(terms[:, 2, :].astype(jnp.float32) - 15.0) / SHY))
+        result = jnp.zeros((rows, HD), jnp.float32)
+        for z in range(in_ref.shape[0]):
+            result += weights[:, z : z + 1] * in_ref[z, y, pl.ds(0, rows), :].astype(jnp.int32).astype(jnp.float32)
+        result = result.astype(jnp.bfloat16)
+        for h in range(heads):
+            out_ref[:, pl.ds((y * heads + h) * HD, HD)] = result[h * tok : (h + 1) * tok, :]
+
+
+def combine(partial, tok, together=4):
     planes, parts, depth, _ = partial.shape
     width = (depth - TERMS) // tok * HD
     return pl.pallas_call(
         functools.partial(combine_kernel, tok),
         out_shape=jax.ShapeDtypeStruct((tok, parts * width), jnp.bfloat16),
-        grid=(parts,),
-        in_specs=[pl.BlockSpec((planes, 1, depth, HD), lambda y: (0, y, 0, 0))],
-        out_specs=pl.BlockSpec((tok, width), lambda y: (0, y)),
+        grid=(parts // together,),
+        in_specs=[pl.BlockSpec((planes, together, depth, HD), lambda y: (0, y, 0, 0))],
+        out_specs=pl.BlockSpec((tok, together * width), lambda y: (0, y)),
         name="combine",
     )(partial)
 
@@ -265,7 +267,8 @@
     rows = parts * heads * tok
     q = jnp.concatenate([fresh[:, : heads * tok].reshape(rows, HD), lists], axis=0)
     q, near_left, near_right = lax.optimization_barrier((q, left[0], right[1]))
-    q = lax.all_gather(q, "z", axis=0, tiled=False)
+    q = jnp.broadcast_to(q[None], (planes, *q.shape))
+    q = lax.all_to_all(q, "z", split_axis=0, concat_axis=0, tiled=True)
     own_other, left_other, right_other, far_other = (
         [lax.ppermute(a, "c", swap) for a in pair] for pair in (own, (near_left, left[1]), (right[0], near_right), far)
     )

time: 229 us -> 224 us (0.978)
  the two profiles are of different devices: /device:TPU:6 before, /device:TPU:27 now
where the time goes in v4:
time: 224 us; the launch traced here: 223 us
  blocking collectives  80.5 us (36%)
  starting transfers between devices  56.1 us (25%)
  waiting for transfers between devices  43.9 us (20%)
  Pallas kernels  32.2 us (14%)
  local copies, waits for them, and re-layouts  6.31 us (3%)
  other arithmetic  2.99 us (1%)
    all_to_all x1, blocking collectives, local(): lax.all_to_all(partial, ('z', 'y'), split_axis=0, concat_axis=0, tiled=True)  80.5 us
    pallas_call x1, Pallas kernels, attend(): pl.pallas_call(functools.partial(attend_kernel, len(stores), cap, parts),...  28.6 us
    ppermute x8, starting transfers between devices, local(): lax.ppermute(a, 'c', swap)  23.5 us
    ppermute x2, waiting for transfers between devices, local(): far = [lax.ppermute(left[0], 'x', up), lax.ppermute(right[1], 'x', down)]  16.2 us
    ppermute x1, waiting for transfers between devices, local(): right[0] = lax.ppermute(own[0], 'x', down)  12.6 us
    all_to_all x1, starting transfers between devices, local(): q = lax.all_to_all(q, 'z', split_axis=0, concat_axis=0, tiled=True)  10 us
    all_to_all x1, waiting for transfers between devices, local(): fresh = lax.all_to_all(fresh, 'y', split_axis=0, concat_axis=0, tiled=True)  7.83 us
    all_to_all x1, starting transfers between devices, local(): fresh = lax.all_to_all(fresh, 'y', split_axis=0, concat_axis=0, tiled=True)  6.76 us
  transfers between devices with their start and end apart: 16, of which 7 were waited for; matrix products, arithmetic and copies ran while one was open for 2% of the time, Pallas kernels for 0%

profile of v4, /device:TPU:27, one launch (start us, length us, event | category | flops | bytes accessed | tf_op | source)
XLA Modules:
  0.0 223.1 jit_solution(17334102729114907057)
XLA Ops:
  0.0 2.8 %fusion.22 = (bf16[16,128,2,128]{3,2,1,0:T(2,128)(2,1)S(1)}, bf16[16,128,2,128]{3,2,1,0:T(2,128)(2,1)S(1)}) fusion(bf16[32,128,2,128]{3,2,1,0:T(2,128)(2,1)} %param.10), kind=kLoop, calls=%fused_computation.61 | loop fusion | bytes 4194304 | tf_op jit(solution)/shard_map/slice | solution.py:248
  2.8 0.2 copy.37
  3.1 3.1 %collective-permute-start = (bf16[16,2,128,128]{3,2,1,0:T(8,128)(2,1)S(1)}, bf16[16,2,128,128]{3,2,1,0:T(8,128)(2,1)}, u32[]{:S(2)}, u32[]{:S(2)}) collective-permute-start(bf16[16,2,128,128]{3,2,1,0:T(8,128)(2,1)S(1)} %bitcast.42), channel_id=1, source_target_pairs={{0,128},{128,256},{256,384},{384,0},{1,129},{129,257},{257,385},{3... | collective-permute-start | bytes 3145736 | tf_op jit(solution)/shard_map/ppermute | solution.py:251
  6.5 2.2 collective-permute-start.1
  9.0 0.8 pad_maximum_fusion
  9.7 6.8 %all-to-all-start = ((bf16[8,160,128]{2,1,0:T(8,128)(2,1)}), bf16[8,160,128]{2,1,0:T(8,128)(2,1)S(1)}, u32[]{:S(2)}, u32[]{:S(2)}) async-start(bf16[8,160,128]{2,1,0:T(8,128)(2,1)} %pad_maximum_fusion), calls=%async_computation | async-start | bytes 655360 | tf_op jit(solution)/shard_map/all_to_all | solution.py:264
  17.3 7.8 %all-to-all-done.refs_17_.refs_18_ = bf16[8,160,128]{2,1,0:T(8,128)(2,1)S(1)} async-done(((bf16[8,160,128]{2,1,0:T(8,128)(2,1)}), bf16[8,160,128]{2,1,0:T(8,128)(2,1)S(1)}, u32[]{:S(2)}, u32[]{:S(2)}) %all-to-all-start) | async-done | bytes 327712 | tf_op jit(solution)/shard_map/all_to_all | solution.py:264
  25.2 3.9 %collective-permute-done.refs_12_ = bf16[16,2,128,128]{3,2,1,0:T(8,128)(2,1)} collective-permute-done((bf16[16,2,128,128]{3,2,1,0:T(8,128)(2,1)S(1)}, bf16[16,2,128,128]{3,2,1,0:T(8,128)(2,1)}, u32[]{:S(2)}, u32[]{:S(2)}) %collective-permute-start) | collective-permute-done | bytes 1048608 | tf_op jit(solution)/shard_map/ppermute | solution.py:251
  29.1 3.1 %collective-permute-done.1.refs_5_ = bf16[16,2,128,128]{3,2,1,0:T(8,128)(2,1)} collective-permute-done((bf16[16,2,128,128]{3,2,1,0:T(8,128)(2,1)S(1)}, bf16[16,2,128,128]{3,2,1,0:T(8,128)(2,1)}, u32[]{:S(2)}, u32[]{:S(2)}) %collective-permute-start.1) | collective-permute-done | bytes 1048608 | tf_op jit(solution)/shard_map/ppermute | solution.py:252
  32.2 1.6 broadcast_in_dim.10
  33.8 10.0 %all-to-all-start.1 = ((bf16[8,1032,128]{2,1,0:T(8,128)(2,1)}), bf16[8,1032,128]{2,1,0:T(8,128)(2,1)S(1)}, u32[]{:S(2)}, u32[]{:S(2)}) async-start(bf16[8,1032,128]{2,1,0:T(8,128)(2,1)} %broadcast_in_dim.10), calls=%async_computation.1 | async-start | bytes 4227072 | tf_op jit(solution)/shard_map/all_to_all | solution.py:271
  43.9 2.2 collective-permute-start.4
  46.0 4.3 %collective-permute-start.2 = (bf16[16,2,128,128]{3,2,1,0:T(8,128)(2,1)S(1)}, bf16[16,2,128,128]{3,2,1,0:T(8,128)(2,1)S(1)}, u32[]{:S(2)}, u32[]{:S(2)}) collective-permute-start(bf16[16,2,128,128]{3,2,1,0:T(8,128)(2,1)S(1)} %bitcast.44), channel_id=1, source_target_pairs={{0,8},{8,0},{1,9},{9,1},{2,10},{10,2},{3,11},{11,3},{4,12},{12,4},... | collective-permute-start | bytes 3145736 | tf_op jit(solution)/shard_map/ppermute | solution.py:273
  50.4 3.1 %collective-permute-start.11 = (bf16[16,2,128,128]{3,2,1,0:T(8,128)(2,1)}, bf16[16,2,128,128]{3,2,1,0:T(8,128)(2,1)}, u32[]{:S(2)}, u32[]{:S(2)}) collective-permute-start(bf16[16,2,128,128]{3,2,1,0:T(8,128)(2,1)} %bitcast.47), channel_id=1, source_target_pairs={{0,128},{128,256},{256,384},{384,0},{1,129},{129,257},{257,385},{3... | collective-permute-start | bytes 3145736 | tf_op jit(solution)/shard_map/ppermute | solution.py:253
  53.5 2.2 collective-permute-start.3
  55.7 12.6 %collective-permute-done.4.refs_4_ = bf16[16,2,128,128]{3,2,1,0:T(8,128)(2,1)} collective-permute-done((bf16[16,2,128,128]{3,2,1,0:T(8,128)(2,1)S(1)}, bf16[16,2,128,128]{3,2,1,0:T(8,128)(2,1)}, u32[]{:S(2)}, u32[]{:S(2)}) %collective-permute-start.4) | collective-permute-done | bytes 1048608 | tf_op jit(solution)/shard_map/ppermute | solution.py:254
  68.4 5.0 %collective-permute-start.5 = (bf16[16,2,128,128]{3,2,1,0:T(8,128)(2,1)}, bf16[16,2,128,128]{3,2,1,0:T(8,128)(2,1)}, u32[]{:S(2)}, u32[]{:S(2)}) collective-permute-start(bf16[16,2,128,128]{3,2,1,0:T(8,128)(2,1)} %collective-permute-done.4.refs_4_), channel_id=1, source_target_pairs={{0,8},{8,0},{1,9},{9,1},{2,10},{10,2},{3,11},{11,3},{4,12},{12,4},... | collective-permute-start | bytes 3145736 | tf_op jit(solution)/shard_map/ppermute | solution.py:273
  73.3 2.8 %collective-permute-start.7 = (bf16[16,2,128,128]{3,2,1,0:T(8,128)(2,1)}, bf16[16,2,128,128]{3,2,1,0:T(8,128)(2,1)}, u32[]{:S(2)}, u32[]{:S(2)}) collective-permute-start(bf16[16,2,128,128]{3,2,1,0:T(8,128)(2,1)} %collective-permute-done.refs_12_), channel_id=1, source_target_pairs={{0,128},{128,256},{256,384},{384,0},{1,129},{129,257},{257,385},{3... | collective-permute-start | bytes 3145736 | tf_op jit(solution)/shard_map/ppermute | solution.py:255
  76.2 1.0 copy-done.4
  77.2 2.4 %collective-permute-start.8 = (bf16[16,2,128,128]{3,2,1,0:T(8,128)(2,1)}, bf16[16,2,128,128]{3,2,1,0:T(8,128)(2,1)S(1)}, u32[]{:S(2)}, u32[]{:S(2)}) collective-permute-start(bf16[16,2,128,128]{3,2,1,0:T(8,128)(2,1)} %collective-permute-done.1.refs_5_), channel_id=1, source_target_pairs={{0,384},{128,0},{256,128},{384,256},{1,385},{129,1},{257,129},{385... | collective-permute-start | bytes 3145736 | tf_op jit(solution)/shard_map/ppermute | solution.py:255
  79.7 2.5 %collective-permute-start.6 = (bf16[16,2,128,128]{3,2,1,0:T(8,128)(2,1)}, bf16[16,2,128,128]{3,2,1,0:T(8,128)(2,1)}, u32[]{:S(2)}, u32[]{:S(2)}) collective-permute-start(bf16[16,2,128,128]{3,2,1,0:T(8,128)(2,1)} %collective-permute-done.1.refs_5_), channel_id=1, source_target_pairs={{0,8},{8,0},{1,9},{9,1},{2,10},{10,2},{3,11},{11,3},{4,12},{12,4},... | collective-permute-start | bytes 3145736 | tf_op jit(solution)/shard_map/ppermute | solution.py:273
  82.2 1.9 collective-permute-start.12
  84.1 2.4 %collective-permute-start.13 = (bf16[16,2,128,128]{3,2,1,0:T(8,128)(2,1)}, bf16[16,2,128,128]{3,2,1,0:T(8,128)(2,1)}, u32[]{:S(2)}, u32[]{:S(2)}) collective-permute-start(bf16[16,2,128,128]{3,2,1,0:T(8,128)(2,1)} %collective-permute-done.11.refs_13_), channel_id=1, source_target_pairs={{0,8},{8,0},{1,9},{9,1},{2,10},{10,2},{3,11},{11,3},{4,12},{12,4},... | collective-permute-start | bytes 3145736 | tf_op jit(solution)/shard_map/ppermute | solution.py:273
  86.6 14.7 %collective-permute-done.7.refs_8_ = bf16[16,2,128,128]{3,2,1,0:T(8,128)(2,1)} collective-permute-done((bf16[16,2,128,128]{3,2,1,0:T(8,128)(2,1)}, bf16[16,2,128,128]{3,2,1,0:T(8,128)(2,1)}, u32[]{:S(2)}, u32[]{:S(2)}) %collective-permute-start.7) | collective-permute-done | bytes 1048608 | tf_op jit(solution)/shard_map/ppermute | solution.py:255
  101.3 2.5 %collective-permute-start.9 = (bf16[16,2,128,128]{3,2,1,0:T(8,128)(2,1)}, bf16[16,2,128,128]{3,2,1,0:T(8,128)(2,1)}, u32[]{:S(2)}, u32[]{:S(2)}) collective-permute-start(bf16[16,2,128,128]{3,2,1,0:T(8,128)(2,1)} %collective-permute-done.7.refs_8_), channel_id=1, source_target_pairs={{0,8},{8,0},{1,9},{9,1},{2,10},{10,2},{3,11},{11,3},{4,12},{12,4},... | collective-permute-start | bytes 3145736 | tf_op jit(solution)/shard_map/ppermute | solution.py:273
  103.7 1.5 collective-permute-done.8.refs_9_
  105.3 2.7 %collective-permute-start.10 = (bf16[16,2,128,128]{3,2,1,0:T(8,128)(2,1)S(1)}, bf16[16,2,128,128]{3,2,1,0:T(8,128)(2,1)}, u32[]{:S(2)}, u32[]{:S(2)}) collective-permute-start(bf16[16,2,128,128]{3,2,1,0:T(8,128)(2,1)S(1)} %collective-permute-done.8.refs_9_), channel_id=1, source_target_pairs={{0,8},{8,0},{1,9},{9,1},{2,10},{10,2},{3,11},{11,3},{4,12},{12,4},... | collective-permute-start | bytes 3145736 | tf_op jit(solution)/shard_map/ppermute | solution.py:273
  108.2 0.9 convert_reduce_fusion.1
  109.4 0.8 select_reduce_fusion.item_ref
  110.4 28.6 %attend.1 = s16[64,136,128]{2,1,0:T(8,128)(2,1)} custom-call(s32[8,16]{1,0:T(8,128)} %select_reduce_fusion.item_ref, s32[8]{0:T(128)} %get-tuple-element.11.count_ref, s32[1]{0:T(128)} %bitcast.12.home_ref, bf16[16,2,128,128]{3,2,1,0:T(8,128)(2,1)} %bitcast.45, bf16[16,2,128,128]{3,2,1,0:T(8,128)(2,1)} %bitcast.49, bf16[16,2,128,128]{3,2,1,0:T(8,128)(2,1)} %copy-done.4, ...), custom_call_target="tpu_custom_call" | custom-call | flops 4294967296 | bytes 8388608 | tf_op jit(solution)/shard_map/attend/pallas_call | solution.py:171
  138.9 80.5 %all_to_all.15 = s16[64,136,128]{2,1,0:T(8,128)(2,1)} all-to-all(s16[64,136,128]{2,1,0:T(8,128)(2,1)} %attend.1), channel_id=1, replica_groups=mesh['x'=4,'z'=8,'c'=2,'y'=8] {'z','y'}, dimensions={0} | all-to-all | bytes 4456448 | tf_op jit(solution)/shard_map/all_to_all | solution.py:285
  219.4 3.7 %combine.1 = bf16[16,8192]{1,0:T(8,128)(2,1)} custom-call(s16[8,8,136,128]{3,2,1,0:T(8,128)(2,1)} %bitcast.41), custom_call_target="tpu_custom_call" | custom-call | tf_op jit(solution)/shard_map/combine/pallas_call | solution.py:219
  (50 shorter events, 1.3 us)
Async XLA Ops:
  2.8 5.9 %copy-start.7 = (bf16[16,1024]{1,0:T(8,128)(2,1)S(1)}, bf16[16,1024]{1,0:T(8,128)(2,1)}, u32[]{:S(2)}) copy-start(bf16[16,1024]{1,0:T(8,128)(2,1)} %param.8) | copy-start | bytes 98308
  2.8 5.9 %copy-start.8 = (bf16[16,1024]{1,0:T(8,128)(2,1)S(1)}, bf16[16,1024]{1,0:T(8,128)(2,1)}, u32[]{:S(2)}) copy-start(bf16[16,1024]{1,0:T(8,128)(2,1)} %param.9) | copy-start | bytes 98308
  2.8 5.9 %copy-start.6 = (bf16[16,8192]{1,0:T(8,128)(2,1)S(1)}, bf16[16,8192]{1,0:T(8,128)(2,1)}, u32[]{:S(2)}) copy-start(bf16[16,8192]{1,0:T(8,128)(2,1)} %param.7) | copy-start | bytes 786436
  3.1 42.9 %copy-start.2 = (bf16[16,128,2,128]{3,1,2,0:T(8,128)(2,1)}, bf16[16,128,2,128]{3,1,2,0:T(8,128)(2,1)S(1)}, u32[]{:S(2)}) copy-start(bf16[16,128,2,128]{3,1,2,0:T(8,128)(2,1)S(1)} %copy.37) | copy-start | bytes 3145732
  3.1 26.0 %collective-permute-start = (bf16[16,2,128,128]{3,2,1,0:T(8,128)(2,1)S(1)}, bf16[16,2,128,128]{3,2,1,0:T(8,128)(2,1)}, u32[]{:S(2)}, u32[]{:S(2)}) collective-permute-start(bf16[16,2,128,128]{3,2,1,0:T(8,128)(2,1)S(1)} %bitcast.42), channel_id=1, source_target_pairs={{0,128},{128,256},{256,384},{384,0},{1,129},{129,257},{257,385},{3... | collective-permute-start | bytes 3145736 | tf_op jit(solution)/shard_map/ppermute | solution.py:251
  6.2 10.9 %copy-start.9 = (s32[1,64]{1,0:T(1,128)S(1)}, s32[1,64]{1,0:T(1,128)}, u32[]{:S(2)}) copy-start(s32[1,64]{1,0:T(1,128)} %param.12) | copy-start | bytes 772
  6.2 11.0 %copy-start.10 = (s32[1,64,1]{1,2,0:T(1,128)S(1)}, s32[1,64,1]{1,2,0:T(1,128)}, u32[]{:S(2)}) copy-start(s32[1,64,1]{1,2,0:T(1,128)} %param.11) | copy-start | bytes 772
  6.5 27.3 %copy-start.3 = (bf16[16,128,2,128]{3,1,2,0:T(8,128)(2,1)}, bf16[16,128,2,128]{3,1,2,0:T(8,128)(2,1)S(1)}, u32[]{:S(2)}) copy-start(bf16[16,128,2,128]{3,1,2,0:T(8,128)(2,1)S(1)} %copy.36) | copy-start | bytes 3145732
  6.5 25.7 %collective-permute-start.1 = (bf16[16,2,128,128]{3,2,1,0:T(8,128)(2,1)S(1)}, bf16[16,2,128,128]{3,2,1,0:T(8,128)(2,1)}, u32[]{:S(2)}, u32[]{:S(2)}) collective-permute-start(bf16[16,2,128,128]{3,2,1,0:T(8,128)(2,1)S(1)} %bitcast.46), channel_id=1, source_target_pairs={{0,384},{128,0},{256,128},{384,256},{1,385},{129,1},{257,129},{385... | collective-permute-start | bytes 3145736 | tf_op jit(solution)/shard_map/ppermute | solution.py:252
  9.7 15.4 %all-to-all-start = ((bf16[8,160,128]{2,1,0:T(8,128)(2,1)}), bf16[8,160,128]{2,1,0:T(8,128)(2,1)S(1)}, u32[]{:S(2)}, u32[]{:S(2)}) async-start(bf16[8,160,128]{2,1,0:T(8,128)(2,1)} %pad_maximum_fusion), calls=%async_computation | async-start | bytes 655360 | tf_op jit(solution)/shard_map/all_to_all | solution.py:264
  25.1 8.7 %copy-start.1 = (bf16[8,160,128]{2,1,0:T(8,128)(2,1)}, bf16[8,160,128]{2,1,0:T(8,128)(2,1)S(1)}, u32[]{:S(2)}) copy-start(bf16[8,160,128]{2,1,0:T(8,128)(2,1)S(1)} %all-to-all-done.refs_17_.refs_18_) | copy-start | bytes 983044
  33.8 74.2 %all-to-all-start.1 = ((bf16[8,1032,128]{2,1,0:T(8,128)(2,1)}), bf16[8,1032,128]{2,1,0:T(8,128)(2,1)S(1)}, u32[]{:S(2)}, u32[]{:S(2)}) async-start(bf16[8,1032,128]{2,1,0:T(8,128)(2,1)} %broadcast_in_dim.10), calls=%async_computation.1 | async-start | bytes 4227072 | tf_op jit(solution)/shard_map/all_to_all | solution.py:271
  43.9 24.5 %collective-permute-start.4 = (bf16[16,2,128,128]{3,2,1,0:T(8,128)(2,1)S(1)}, bf16[16,2,128,128]{3,2,1,0:T(8,128)(2,1)}, u32[]{:S(2)}, u32[]{:S(2)}) collective-permute-start(bf16[16,2,128,128]{3,2,1,0:T(8,128)(2,1)S(1)} %bitcast.43), channel_id=1, source_target_pairs={{0,384},{128,0},{256,128},{384,256},{1,385},{129,1},{257,129},{385... | collective-permute-start | bytes 3145736 | tf_op jit(solution)/shard_map/ppermute | solution.py:254
  46.0 30.1 %collective-permute-start.2 = (bf16[16,2,128,128]{3,2,1,0:T(8,128)(2,1)S(1)}, bf16[16,2,128,128]{3,2,1,0:T(8,128)(2,1)S(1)}, u32[]{:S(2)}, u32[]{:S(2)}) collective-permute-start(bf16[16,2,128,128]{3,2,1,0:T(8,128)(2,1)S(1)} %bitcast.44), channel_id=1, source_target_pairs={{0,8},{8,0},{1,9},{9,1},{2,10},{10,2},{3,11},{11,3},{4,12},{12,4},... | collective-permute-start | bytes 3145736 | tf_op jit(solution)/shard_map/ppermute | solution.py:273
  50.4 29.3 %collective-permute-start.11 = (bf16[16,2,128,128]{3,2,1,0:T(8,128)(2,1)}, bf16[16,2,128,128]{3,2,1,0:T(8,128)(2,1)}, u32[]{:S(2)}, u32[]{:S(2)}) collective-permute-start(bf16[16,2,128,128]{3,2,1,0:T(8,128)(2,1)} %bitcast.47), channel_id=1, source_target_pairs={{0,128},{128,256},{256,384},{384,0},{1,129},{129,257},{257,385},{3... | collective-permute-start | bytes 3145736 | tf_op jit(solution)/shard_map/ppermute | solution.py:253
  53.5 28.7 %collective-permute-start.3 = (bf16[16,2,128,128]{3,2,1,0:T(8,128)(2,1)}, bf16[16,2,128,128]{3,2,1,0:T(8,128)(2,1)}, u32[]{:S(2)}, u32[]{:S(2)}) collective-permute-start(bf16[16,2,128,128]{3,2,1,0:T(8,128)(2,1)} %bitcast.48), channel_id=1, source_target_pairs={{0,8},{8,0},{1,9},{9,1},{2,10},{10,2},{3,11},{11,3},{4,12},{12,4},... | collective-permute-start | bytes 3145736 | tf_op jit(solution)/shard_map/ppermute | solution.py:273
  68.4 15.8 %collective-permute-start.5 = (bf16[16,2,128,128]{3,2,1,0:T(8,128)(2,1)}, bf16[16,2,128,128]{3,2,1,0:T(8,128)(2,1)}, u32[]{:S(2)}, u32[]{:S(2)}) collective-permute-start(bf16[16,2,128,128]{3,2,1,0:T(8,128)(2,1)} %collective-permute-done.4.refs_4_), channel_id=1, source_target_pairs={{0,8},{8,0},{1,9},{9,1},{2,10},{10,2},{3,11},{11,3},{4,12},{12,4},... | collective-permute-start | bytes 3145736 | tf_op jit(solution)/shard_map/ppermute | solution.py:273
  73.3 27.9 %collective-permute-start.7 = (bf16[16,2,128,128]{3,2,1,0:T(8,128)(2,1)}, bf16[16,2,128,128]{3,2,1,0:T(8,128)(2,1)}, u32[]{:S(2)}, u32[]{:S(2)}) collective-permute-start(bf16[16,2,128,128]{3,2,1,0:T(8,128)(2,1)} %collective-permute-done.refs_12_), channel_id=1, source_target_pairs={{0,128},{128,256},{256,384},{384,0},{1,129},{129,257},{257,385},{3... | collective-permute-start | bytes 3145736 | tf_op jit(solution)/shard_map/ppermute | solution.py:255
  76.2 1.1 copy-start.4
  77.2 28.0 %collective-permute-start.8 = (bf16[16,2,128,128]{3,2,1,0:T(8,128)(2,1)}, bf16[16,2,128,128]{3,2,1,0:T(8,128)(2,1)S(1)}, u32[]{:S(2)}, u32[]{:S(2)}) collective-permute-start(bf16[16,2,128,128]{3,2,1,0:T(8,128)(2,1)} %collective-permute-done.1.refs_5_), channel_id=1, source_target_pairs={{0,384},{128,0},{256,128},{384,256},{1,385},{129,1},{257,129},{385... | collective-permute-start | bytes 3145736 | tf_op jit(solution)/shard_map/ppermute | solution.py:255
  79.7 30.5 %collective-permute-start.6 = (bf16[16,2,128,128]{3,2,1,0:T(8,128)(2,1)}, bf16[16,2,128,128]{3,2,1,0:T(8,128)(2,1)}, u32[]{:S(2)}, u32[]{:S(2)}) collective-permute-start(bf16[16,2,128,128]{3,2,1,0:T(8,128)(2,1)} %collective-permute-done.1.refs_5_), channel_id=1, source_target_pairs={{0,8},{8,0},{1,9},{9,1},{2,10},{10,2},{3,11},{11,3},{4,12},{12,4},... | collective-permute-start | bytes 3145736 | tf_op jit(solution)/shard_map/ppermute | solution.py:273
  82.2 28.0 %collective-permute-start.12 = (bf16[16,2,128,128]{3,2,1,0:T(8,128)(2,1)}, bf16[16,2,128,128]{3,2,1,0:T(8,128)(2,1)}, u32[]{:S(2)}, u32[]{:S(2)}) collective-permute-start(bf16[16,2,128,128]{3,2,1,0:T(8,128)(2,1)} %collective-permute-done.refs_12_), channel_id=1, source_target_pairs={{0,8},{8,0},{1,9},{9,1},{2,10},{10,2},{3,11},{11,3},{4,12},{12,4},... | collective-permute-start | bytes 3145736 | tf_op jit(solution)/shard_map/ppermute | solution.py:273
  84.1 26.1 %collective-permute-start.13 = (bf16[16,2,128,128]{3,2,1,0:T(8,128)(2,1)}, bf16[16,2,128,128]{3,2,1,0:T(8,128)(2,1)}, u32[]{:S(2)}, u32[]{:S(2)}) collective-permute-start(bf16[16,2,128,128]{3,2,1,0:T(8,128)(2,1)} %collective-permute-done.11.refs_13_), channel_id=1, source_target_pairs={{0,8},{8,0},{1,9},{9,1},{2,10},{10,2},{3,11},{11,3},{4,12},{12,4},... | collective-permute-start | bytes 3145736 | tf_op jit(solution)/shard_map/ppermute | solution.py:273
  101.3 9.0 %collective-permute-start.9 = (bf16[16,2,128,128]{3,2,1,0:T(8,128)(2,1)}, bf16[16,2,128,128]{3,2,1,0:T(8,128)(2,1)}, u32[]{:S(2)}, u32[]{:S(2)}) collective-permute-start(bf16[16,2,128,128]{3,2,1,0:T(8,128)(2,1)} %collective-permute-done.7.refs_8_), channel_id=1, source_target_pairs={{0,8},{8,0},{1,9},{9,1},{2,10},{10,2},{3,11},{11,3},{4,12},{12,4},... | collective-permute-start | bytes 3145736 | tf_op jit(solution)/shard_map/ppermute | solution.py:273
  105.3 5.1 %copy-start.5 = (bf16[16,2,128,128]{3,2,1,0:T(8,128)(2,1)}, bf16[16,2,128,128]{3,2,1,0:T(8,128)(2,1)S(1)}, u32[]{:S(2)}) copy-start(bf16[16,2,128,128]{3,2,1,0:T(8,128)(2,1)S(1)} %collective-permute-done.8.refs_9_) | copy-start | bytes 3145732
  105.3 5.1 %collective-permute-start.10 = (bf16[16,2,128,128]{3,2,1,0:T(8,128)(2,1)S(1)}, bf16[16,2,128,128]{3,2,1,0:T(8,128)(2,1)}, u32[]{:S(2)}, u32[]{:S(2)}) collective-permute-start(bf16[16,2,128,128]{3,2,1,0:T(8,128)(2,1)S(1)} %collective-permute-done.8.refs_9_), channel_id=1, source_target_pairs={{0,8},{8,0},{1,9},{9,1},{2,10},{10,2},{3,11},{11,3},{4,12},{12,4},... | collective-permute-start | bytes 3145736 | tf_op jit(solution)/shard_map/ppermute | solution.py:273
  108.0 2.3 %copy-start = (bf16[8,1032,128]{2,1,0:T(8,128)(2,1)}, bf16[8,1032,128]{2,1,0:T(8,128)(2,1)S(1)}, u32[]{:S(2)}) copy-start(bf16[8,1032,128]{2,1,0:T(8,128)(2,1)S(1)} %all-to-all-done.1.refs_16_) | copy-start | bytes 6340612
